TPU v7x, 32 devices: a whole 2x2x4 slice. The times are simulated.
32 devices in a mesh: groups: 2 (over y), seq: 4 (over z), head: 2 (over x), rep: 2 (over core).
Axes of the slice: x: 2, y: 2, z: 4, core: 2. Of those that a mesh axis runs over, the one named last changes fastest.
Arguments:
- queries: bfloat16 [32768, 16, 128], P(('groups', 'seq'), ('head', 'rep')), parts along dimension 0, may hold values from -8 to 8
- keys: bfloat16 [32768, 128], P(('groups', 'seq')), parts along dimension 0, may hold values from -6 to 6
- values: bfloat16 [32768, 128], P(('groups', 'seq')), parts along dimension 0, may hold values from -6 to 6
- query_maps: bfloat16 [32, 128, 128], P(('groups', 'head', 'rep')), parts along dimension 0, may hold values from -0.5 to 0.5
- key_map: bfloat16 [256, 128], P('groups'), parts along dimension 0, may hold values from -0.046875 to 0.046875
- linear_cotangent: bfloat16 [32768, 16, 128], P(('groups', 'seq'), ('head', 'rep')), parts along dimension 0, may hold values from -0.046875 to 0.046875
Outputs:
- softmax_out: bfloat16 [32768, 16, 128], P(('groups', 'seq'), ('head', 'rep')), parts along dimension 0
- linear_out: bfloat16 [32768, 16, 128], P(('groups', 'seq'), ('head', 'rep')), parts along dimension 0
- map_gradient: float32 [256, 16, 128], P(('groups', 'seq'), ('head', 'rep')), parts along dimension 0
There are 2 independent parts, one for each index of `groups`. A program takes and returns all parts, laid end to end along the dimension named above; each array names one. Nothing has to cross between parts.
All inputs are finite; a program needn't handle non-finite values.
Results may differ from a plain program's by a relative error of at most 0.0058.
Values may be sent and summed in bfloat16 or wider, within the bound.
A program may use at most 128 MiB of HBM per device.

v0:
```python
import jax
import jax.numpy as jnp
from jax import lax
from jax.sharding import PartitionSpec as P

W = 512


def from_behind(value, axis, steps):
    count = lax.axis_size(axis)
    leading, last = (max(0, -steps), min(count, count - steps))
    return lax.ppermute(value, axis, [(source, source + steps) for source in range(leading, last)])


def carried_in(array, axis, combine, identity):
    count, mine = (lax.axis_size(axis), lax.axis_index(axis))
    everything = lax.all_gather(array, axis)
    start = jnp.broadcast_to(jnp.asarray(identity, array.dtype), array.shape)

    def lap(k, before):
        reached = k < mine
        new = combine(before, everything[k])
        return jnp.where(reached, new, before)

    return lax.fori_loop(0, count, lap, start)


def window_block(block_index, start_state, tensors, position_base):
    queries, keys_ext, values_ext, query_features, key_features, values, cotangent = tensors
    highest_precision = lax.Precision.HIGHEST
    first_row = block_index * W
    head_dim = keys_ext.shape[1]
    query_block = lax.dynamic_slice_in_dim(queries, first_row, W, 0)
    key_window = lax.dynamic_slice_in_dim(keys_ext, first_row, 2 * W, 0)
    value_window = lax.dynamic_slice_in_dim(values_ext, first_row, 2 * W, 0)
    query_pos = position_base + first_row + jnp.arange(W, dtype=jnp.int32)
    key_pos = position_base + first_row - W + jnp.arange(2 * W, dtype=jnp.int32)
    spacing = query_pos[:, None] - key_pos[None, :]
    allowed = (spacing >= 0) & (spacing < W) & (key_pos[None, :] >= 0)
    scores = jnp.einsum(
        "whd,kd->hwk", query_block, key_window, preferred_element_type=jnp.float32
    ) * head_dim ** (-0.5)
    scores = jnp.where(allowed[None], scores, -1e30)
    highest = jnp.max(scores, axis=2, keepdims=True)
    shifted_exp = jnp.exp(scores - highest)
    weights = (shifted_exp / jnp.sum(shifted_exp, axis=2, keepdims=True)).astype(jnp.bfloat16)
    soft_block = jnp.einsum(
        "hwk,kd->whd", weights, value_window, preferred_element_type=jnp.float32
    ).astype(jnp.bfloat16)
    feature_block = lax.dynamic_slice_in_dim(query_features, first_row, W, 0)
    key_block = lax.dynamic_slice_in_dim(key_features, first_row, W, 0)
    value_block = lax.dynamic_slice_in_dim(values, first_row, W, 0)
    cotangent_block = lax.dynamic_slice_in_dim(cotangent, first_row, W, 0)
    causal = jnp.arange(W)[:, None] >= jnp.arange(W)[None, :]
    factor = lax.rsqrt((query_pos + 1).astype(jnp.float32))[:, None, None]
    linear_scores = jnp.where(
        causal[None],
        jnp.einsum("whf,sf->hws", feature_block, key_block, preferred_element_type=jnp.float32),
        0.0,
    ).astype(jnp.bfloat16)
    inside = jnp.einsum(
        "hws,sd->whd", linear_scores, value_block, preferred_element_type=jnp.float32
    )
    carried = jnp.einsum(
        "whf,fd->whd", feature_block.astype(jnp.float32), start_state, precision=highest_precision
    )
    linear_block = (factor * (inside + carried)).astype(jnp.bfloat16)
    back_scores = jnp.where(
        causal[None],
        jnp.einsum("whd,sd->hws", cotangent_block, value_block, preferred_element_type=jnp.float32),
        0.0,
    ).astype(jnp.bfloat16)
    back_inside = jnp.einsum(
        "hws,sf->whf", back_scores, key_block, preferred_element_type=jnp.float32
    )
    back_carried = jnp.einsum(
        "whd,fd->whf", cotangent_block.astype(jnp.float32), start_state, precision=highest_precision
    )
    feature_gradient = (factor * (back_inside + back_carried)).astype(jnp.bfloat16)
    return (soft_block, linear_block, feature_gradient)


def per_device(queries, keys, values, query_maps, key_map, linear_cotangent):
    tokens_here = keys.shape[0]
    head_dim = keys.shape[1]
    heads_here = queries.shape[1]
    block_count = tokens_here // W
    seq_rank = lax.axis_index("seq")
    rim_keys, rim_values = from_behind(
        (keys[tokens_here - W :], values[tokens_here - W :]), "seq", 1
    )
    keys_ext = jnp.concatenate([rim_keys, keys], axis=0)
    values_ext = jnp.concatenate([rim_values, values], axis=0)
    key_features = jnp.dot(keys, key_map, preferred_element_type=jnp.float32).astype(jnp.bfloat16)
    query_features = jnp.einsum(
        "thd,hdf->thf", queries, query_maps, preferred_element_type=jnp.float32
    ).astype(jnp.bfloat16)
    block_states = jnp.einsum(
        "bwf,bwd->bfd",
        key_features.reshape(block_count, W, head_dim),
        values.reshape(block_count, W, head_dim),
        preferred_element_type=jnp.float32,
    )
    running = jnp.cumsum(block_states, axis=0)
    local_sum = running[-1]
    within_device = jnp.concatenate([jnp.zeros_like(block_states[:1]), running[:-1]], axis=0)
    zero_state = jnp.zeros((head_dim, head_dim), jnp.float32)

    def combine_states(earlier, later):
        return earlier + later

    prefix = carried_in(local_sum, "seq", combine_states, zero_state)
    starts = prefix[None] + within_device
    tensors = (
        queries,
        keys_ext,
        values_ext,
        query_features,
        key_features,
        values,
        linear_cotangent,
    )
    position_base = seq_rank * tokens_here

    def one_block(block_item):
        return window_block(block_item[0], block_item[1], tensors, position_base)

    soft_parts, linear_parts, gradient_parts = lax.map(
        one_block, (jnp.arange(block_count, dtype=jnp.int32), starts)
    )
    softmax_out = soft_parts.reshape(tokens_here, heads_here, head_dim)
    linear_out = linear_parts.reshape(tokens_here, heads_here, head_dim)
    feature_gradient = gradient_parts.reshape(tokens_here, heads_here, head_dim)
    map_gradient = lax.psum_scatter(
        jnp.einsum("the,thf->ehf", queries, feature_gradient, preferred_element_type=jnp.float32),
        "seq",
        scatter_dimension=0,
        tiled=True,
    )
    return (softmax_out, linear_out, map_gradient)


def solution(mesh):
    return jax.shard_map(
        per_device,
        mesh=mesh,
        in_specs=(
            P(("groups", "seq"), ("head", "rep"), None),
            P(("groups", "seq"), None),
            P(("groups", "seq"), None),
            P(("groups", "head", "rep"), None, None),
            P("groups", None),
            P(("groups", "seq"), ("head", "rep"), None),
        ),
        out_specs=(
            P(("groups", "seq"), ("head", "rep"), None),
            P(("groups", "seq"), ("head", "rep"), None),
            P(("groups", "seq"), ("head", "rep"), None),
        ),
        check_vma=False,
    )
```

profile of v0, /device:TPU:0, one launch (start us, length us, event | category | flops | bytes accessed | tf_op | source)
XLA Modules:
  0.0 301.6 jit_solution(11189853293392144105)
XLA Ops:
  8.8 5.0 %collective-permute-start = (bf16[512,128]{0,1:T(8,128)(2,1)S(1)}, bf16[512,128]{0,1:T(8,128)(2,1)S(1)}, u32[]{:S(2)}, u32[]{:S(2)}) collective-permute-start(bf16[512,128]{0,1:T(8,128)(2,1)S(1)} %slice.16), channel_id=1, source_target_pairs={{0,4},{4,8},{8,12},{1,5},{5,9},{9,13},{2,6},{6,10},{10,14},{3,7},{... | collective-permute-start | bytes 393224 | tf_op jit(solution)/shard_map/ppermute | solution.py:12
  14.7 3.5 %collective-permute-start.1 = (bf16[512,128]{1,0:T(8,128)(2,1)S(1)}, bf16[512,128]{1,0:T(8,128)(2,1)S(1)}, u32[]{:S(2)}, u32[]{:S(2)}) collective-permute-start(bf16[512,128]{1,0:T(8,128)(2,1)S(1)} %slice.13), channel_id=1, source_target_pairs={{0,4},{4,8},{8,12},{1,5},{5,9},{9,13},{2,6},{6,10},{10,14},{3,7},{... | collective-permute-start | bytes 393224 | tf_op jit(solution)/shard_map/ppermute | solution.py:12
  21.4 14.4 %all_gather.3 = f32[4,128,128]{2,1,0:T(8,128)S(1)} all-gather(f32[1,128,128]{2,1,0:T(8,128)S(1)} %slice.17), channel_id=1, replica_groups=mesh['groups'=2,'seq'=4,'head'=2,'rep'=2] {'seq'}, dimensions={0}, use_global_device_ids=true | all-gather | bytes 327680 | tf_op jit(solution)/shard_map/all_gather | solution.py:17
  36.0 4.8 %copy.57 = bf16[4096,4,128]{2,0,1:T(8,128)(2,1)} copy(bf16[4096,4,128]{2,1,0:T(4,128)(2,1)} %param.10) | data formatting | bytes 8388608 | tf_op jit(solution)/shard_map/while | solution.py:128
  40.8 3.2 %fusion.82 = bf16[4096,4,128]{0,2,1:T(8,128)(2,1)} fusion(bf16[4,128,128]{2,1,0:T(8,128)(2,1)S(1)} %copy-done, bf16[4096,4,128]{2,1,0:T(4,128)(2,1)S(1)} %copy-done.1), kind=kOutput, calls=%fused_computation.81 | convolution fusion | flops 538968064 | bytes 8519680 | tf_op jit(solution)/shard_map/thd,hdf->thf/dot_general | solution.py:95
  47.2 205.7 %while.30 = (s32[]{:T(128)}, bf16[8,512,4,128]{3,2,1,0:T(4,128)(2,1)}, bf16[8,512,4,128]{3,2,1,0:T(4,128)(2,1)}, bf16[8,512,4,128]{3,1,0,2:T(8,128)(2,1)}, s32[8...) while((s32[]{:T(128)}, ...), condition=%wide.region_6.7_spmd, body=%wide.region_3.6_spmd.sunk | while | flops 2974291968 | bytes 35562308 | solution.py:128
  49.3 7.5 %fusion.139 = (f32[4,512]{1,0:T(4,128)S(1)}, f32[4,512,1024]{1,2,0:T(8,128)}) fusion(pred[512,1024]{0,1:T(8,128)(4,1)S(1)} %fusion.138, bf16[4096,4,128]{2,0,1:T(8,128)(2,1)} %get-tuple-element.548, s32[]{:T(128)S(6)} %select_n.112, bf16[4608,128]{1,0:T(8,128)(2,1)} %get-tuple-element.547, s32[]{:T(128)S(6)} %select_n.113), kind=kOutput, calls=%fused_computation.90.clone.1 | convolution fusion | flops 545260544 | bytes 9707528 | tf_op jit(solution)/shard_map/while/body/eval_jaxpr/sub | solution.py:45
  56.8 4.2 %fusion.140 = bf16[1,512,4,128]{1,3,2,0:T(8,128)(2,1)S(1)} fusion(f32[4,512,1024]{1,2,0:T(8,128)} %get-tuple-element.474, f32[4,512]{1,0:T(4,128)S(1)} %get-tuple-element.475, bf16[4608,128]{0,1:T(8,128)(2,1)} %get-tuple-element.545, s32[]{:T(128)S(6)} %select_n.113), kind=kOutput, calls=%fused_computation.30.clone.1 | convolution fusion | flops 541327360 | bytes 9183236 | tf_op jit(solution)/shard_map/while/body/eval_jaxpr/hwk,kd->whd/dot_general | solution.py:47
  75.0 7.5 %fusion.139 = (f32[4,512]{1,0:T(4,128)S(1)}, f32[4,512,1024]{1,2,0:T(8,128)}) fusion(pred[512,1024]{0,1:T(8,128)(4,1)S(1)} %fusion.138, bf16[4096,4,128]{2,0,1:T(8,128)(2,1)} %get-tuple-element.548, s32[]{:T(128)S(6)} %select_n.112, bf16[4608,128]{1,0:T(8,128)(2,1)} %get-tuple-element.547, s32[]{:T(128)S(6)} %select_n.113), kind=kOutput, calls=%fused_computation.90.clone.1 | convolution fusion | flops 545260544 | bytes 9707528 | tf_op jit(solution)/shard_map/while/body/eval_jaxpr/sub | solution.py:45
  82.5 4.2 %fusion.140 = bf16[1,512,4,128]{1,3,2,0:T(8,128)(2,1)S(1)} fusion(f32[4,512,1024]{1,2,0:T(8,128)} %get-tuple-element.474, f32[4,512]{1,0:T(4,128)S(1)} %get-tuple-element.475, bf16[4608,128]{0,1:T(8,128)(2,1)} %get-tuple-element.545, s32[]{:T(128)S(6)} %select_n.113), kind=kOutput, calls=%fused_computation.30.clone.1 | convolution fusion | flops 541327360 | bytes 9183236 | tf_op jit(solution)/shard_map/while/body/eval_jaxpr/hwk,kd->whd/dot_general | solution.py:47
  100.8 7.5 %fusion.139 = (f32[4,512]{1,0:T(4,128)S(1)}, f32[4,512,1024]{1,2,0:T(8,128)}) fusion(pred[512,1024]{0,1:T(8,128)(4,1)S(1)} %fusion.138, bf16[4096,4,128]{2,0,1:T(8,128)(2,1)} %get-tuple-element.548, s32[]{:T(128)S(6)} %select_n.112, bf16[4608,128]{1,0:T(8,128)(2,1)} %get-tuple-element.547, s32[]{:T(128)S(6)} %select_n.113), kind=kOutput, calls=%fused_computation.90.clone.1 | convolution fusion | flops 545260544 | bytes 9707528 | tf_op jit(solution)/shard_map/while/body/eval_jaxpr/sub | solution.py:45
  108.2 4.2 %fusion.140 = bf16[1,512,4,128]{1,3,2,0:T(8,128)(2,1)S(1)} fusion(f32[4,512,1024]{1,2,0:T(8,128)} %get-tuple-element.474, f32[4,512]{1,0:T(4,128)S(1)} %get-tuple-element.475, bf16[4608,128]{0,1:T(8,128)(2,1)} %get-tuple-element.545, s32[]{:T(128)S(6)} %select_n.113), kind=kOutput, calls=%fused_computation.30.clone.1 | convolution fusion | flops 541327360 | bytes 9183236 | tf_op jit(solution)/shard_map/while/body/eval_jaxpr/hwk,kd->whd/dot_general | solution.py:47
  126.5 7.5 %fusion.139 = (f32[4,512]{1,0:T(4,128)S(1)}, f32[4,512,1024]{1,2,0:T(8,128)}) fusion(pred[512,1024]{0,1:T(8,128)(4,1)S(1)} %fusion.138, bf16[4096,4,128]{2,0,1:T(8,128)(2,1)} %get-tuple-element.548, s32[]{:T(128)S(6)} %select_n.112, bf16[4608,128]{1,0:T(8,128)(2,1)} %get-tuple-element.547, s32[]{:T(128)S(6)} %select_n.113), kind=kOutput, calls=%fused_computation.90.clone.1 | convolution fusion | flops 545260544 | bytes 9707528 | tf_op jit(solution)/shard_map/while/body/eval_jaxpr/sub | solution.py:45
  133.9 4.2 %fusion.140 = bf16[1,512,4,128]{1,3,2,0:T(8,128)(2,1)S(1)} fusion(f32[4,512,1024]{1,2,0:T(8,128)} %get-tuple-element.474, f32[4,512]{1,0:T(4,128)S(1)} %get-tuple-element.475, bf16[4608,128]{0,1:T(8,128)(2,1)} %get-tuple-element.545, s32[]{:T(128)S(6)} %select_n.113), kind=kOutput, calls=%fused_computation.30.clone.1 | convolution fusion | flops 541327360 | bytes 9183236 | tf_op jit(solution)/shard_map/while/body/eval_jaxpr/hwk,kd->whd/dot_general | solution.py:47
  152.2 7.5 %fusion.139 = (f32[4,512]{1,0:T(4,128)S(1)}, f32[4,512,1024]{1,2,0:T(8,128)}) fusion(pred[512,1024]{0,1:T(8,128)(4,1)S(1)} %fusion.138, bf16[4096,4,128]{2,0,1:T(8,128)(2,1)} %get-tuple-element.548, s32[]{:T(128)S(6)} %select_n.112, bf16[4608,128]{1,0:T(8,128)(2,1)} %get-tuple-element.547, s32[]{:T(128)S(6)} %select_n.113), kind=kOutput, calls=%fused_computation.90.clone.1 | convolution fusion | flops 545260544 | bytes 9707528 | tf_op jit(solution)/shard_map/while/body/eval_jaxpr/sub | solution.py:45
  159.6 4.2 %fusion.140 = bf16[1,512,4,128]{1,3,2,0:T(8,128)(2,1)S(1)} fusion(f32[4,512,1024]{1,2,0:T(8,128)} %get-tuple-element.474, f32[4,512]{1,0:T(4,128)S(1)} %get-tuple-element.475, bf16[4608,128]{0,1:T(8,128)(2,1)} %get-tuple-element.545, s32[]{:T(128)S(6)} %select_n.113), kind=kOutput, calls=%fused_computation.30.clone.1 | convolution fusion | flops 541327360 | bytes 9183236 | tf_op jit(solution)/shard_map/while/body/eval_jaxpr/hwk,kd->whd/dot_general | solution.py:47
  177.9 7.5 %fusion.139 = (f32[4,512]{1,0:T(4,128)S(1)}, f32[4,512,1024]{1,2,0:T(8,128)}) fusion(pred[512,1024]{0,1:T(8,128)(4,1)S(1)} %fusion.138, bf16[4096,4,128]{2,0,1:T(8,128)(2,1)} %get-tuple-element.548, s32[]{:T(128)S(6)} %select_n.112, bf16[4608,128]{1,0:T(8,128)(2,1)} %get-tuple-element.547, s32[]{:T(128)S(6)} %select_n.113), kind=kOutput, calls=%fused_computation.90.clone.1 | convolution fusion | flops 545260544 | bytes 9707528 | tf_op jit(solution)/shard_map/while/body/eval_jaxpr/sub | solution.py:45
  185.4 4.2 %fusion.140 = bf16[1,512,4,128]{1,3,2,0:T(8,128)(2,1)S(1)} fusion(f32[4,512,1024]{1,2,0:T(8,128)} %get-tuple-element.474, f32[4,512]{1,0:T(4,128)S(1)} %get-tuple-element.475, bf16[4608,128]{0,1:T(8,128)(2,1)} %get-tuple-element.545, s32[]{:T(128)S(6)} %select_n.113), kind=kOutput, calls=%fused_computation.30.clone.1 | convolution fusion | flops 541327360 | bytes 9183236 | tf_op jit(solution)/shard_map/while/body/eval_jaxpr/hwk,kd->whd/dot_general | solution.py:47
  203.6 7.5 %fusion.139 = (f32[4,512]{1,0:T(4,128)S(1)}, f32[4,512,1024]{1,2,0:T(8,128)}) fusion(pred[512,1024]{0,1:T(8,128)(4,1)S(1)} %fusion.138, bf16[4096,4,128]{2,0,1:T(8,128)(2,1)} %get-tuple-element.548, s32[]{:T(128)S(6)} %select_n.112, bf16[4608,128]{1,0:T(8,128)(2,1)} %get-tuple-element.547, s32[]{:T(128)S(6)} %select_n.113), kind=kOutput, calls=%fused_computation.90.clone.1 | convolution fusion | flops 545260544 | bytes 9707528 | tf_op jit(solution)/shard_map/while/body/eval_jaxpr/sub | solution.py:45
  211.1 4.2 %fusion.140 = bf16[1,512,4,128]{1,3,2,0:T(8,128)(2,1)S(1)} fusion(f32[4,512,1024]{1,2,0:T(8,128)} %get-tuple-element.474, f32[4,512]{1,0:T(4,128)S(1)} %get-tuple-element.475, bf16[4608,128]{0,1:T(8,128)(2,1)} %get-tuple-element.545, s32[]{:T(128)S(6)} %select_n.113), kind=kOutput, calls=%fused_computation.30.clone.1 | convolution fusion | flops 541327360 | bytes 9183236 | tf_op jit(solution)/shard_map/while/body/eval_jaxpr/hwk,kd->whd/dot_general | solution.py:47
  229.3 7.5 %fusion.139 = (f32[4,512]{1,0:T(4,128)S(1)}, f32[4,512,1024]{1,2,0:T(8,128)}) fusion(pred[512,1024]{0,1:T(8,128)(4,1)S(1)} %fusion.138, bf16[4096,4,128]{2,0,1:T(8,128)(2,1)} %get-tuple-element.548, s32[]{:T(128)S(6)} %select_n.112, bf16[4608,128]{1,0:T(8,128)(2,1)} %get-tuple-element.547, s32[]{:T(128)S(6)} %select_n.113), kind=kOutput, calls=%fused_computation.90.clone.1 | convolution fusion | flops 545260544 | bytes 9707528 | tf_op jit(solution)/shard_map/while/body/eval_jaxpr/sub | solution.py:45
  236.8 4.2 %fusion.140 = bf16[1,512,4,128]{1,3,2,0:T(8,128)(2,1)S(1)} fusion(f32[4,512,1024]{1,2,0:T(8,128)} %get-tuple-element.474, f32[4,512]{1,0:T(4,128)S(1)} %get-tuple-element.475, bf16[4608,128]{0,1:T(8,128)(2,1)} %get-tuple-element.545, s32[]{:T(128)S(6)} %select_n.113), kind=kOutput, calls=%fused_computation.30.clone.1 | convolution fusion | flops 541327360 | bytes 9183236 | tf_op jit(solution)/shard_map/while/body/eval_jaxpr/hwk,kd->whd/dot_general | solution.py:47
  252.8 5.2 %convolution_bitcast_fusion = f32[128,4,128]{0,2,1:T(8,128)S(1)} fusion(bf16[4096,4,128]{2,0,1:T(8,128)(2,1)} %bitcast.165, bf16[4096,4,128]{2,1,0:T(4,128)(2,1)} %param.10), kind=kOutput, calls=%fused_computation.85 | convolution fusion | flops 536870912 | bytes 8650752 | tf_op jit(solution)/shard_map/the,thf->ehf/dot_general | solution.py:135
  260.1 33.2 %all-reduce.4.cloned.1.call-done = f32[128,4,128]{2,1,0:T(4,128)} async-done(((f32[128,4,128]{2,1,0:T(4,128)}), f32[128,4,128]{2,1,0:T(4,128)}) %all-reduce.4.cloned.1.call-update) | async-done | bytes 262160
  (176 shorter events, 118.2 us)
Async XLA Ops:
  7.2 33.7 %copy-start = (bf16[4,128,128]{2,1,0:T(8,128)(2,1)S(1)}, bf16[4,128,128]{2,1,0:T(8,128)(2,1)}, u32[]{:S(2)}) copy-start(bf16[4,128,128]{2,1,0:T(8,128)(2,1)} %param.13) | copy-start | bytes 393220
  7.2 12.7 %copy-start.3 = (bf16[4096,128]{1,0:T(8,128)(2,1)S(1)}, bf16[4096,128]{1,0:T(8,128)(2,1)}, u32[]{:S(2)}) copy-start(bf16[4096,128]{1,0:T(8,128)(2,1)} %param.12) | copy-start | bytes 3145732
  7.2 286.1 %all-reduce.4.cloned.1.call-start = ((), (), s32[]{:S(2)}) async-start(), calls=%async_computation | async-start | bytes 524288
  8.8 36.1 %collective-permute-start = (bf16[512,128]{0,1:T(8,128)(2,1)S(1)}, bf16[512,128]{0,1:T(8,128)(2,1)S(1)}, u32[]{:S(2)}, u32[]{:S(2)}) collective-permute-start(bf16[512,128]{0,1:T(8,128)(2,1)S(1)} %slice.16), channel_id=1, source_target_pairs={{0,4},{4,8},{8,12},{1,5},{5,9},{9,13},{2,6},{6,10},{10,14},{3,7},{... | collective-permute-start | bytes 393224 | tf_op jit(solution)/shard_map/ppermute | solution.py:12
  14.7 31.3 %collective-permute-start.1 = (bf16[512,128]{1,0:T(8,128)(2,1)S(1)}, bf16[512,128]{1,0:T(8,128)(2,1)S(1)}, u32[]{:S(2)}, u32[]{:S(2)}) collective-permute-start(bf16[512,128]{1,0:T(8,128)(2,1)S(1)} %slice.13), channel_id=1, source_target_pairs={{0,4},{4,8},{8,12},{1,5},{5,9},{9,13},{2,6},{6,10},{10,14},{3,7},{... | collective-permute-start | bytes 393224 | tf_op jit(solution)/shard_map/ppermute | solution.py:12
  19.9 1.0 copy-start.4
  36.0 4.8 %copy-start.1 = (bf16[4096,4,128]{2,1,0:T(4,128)(2,1)S(1)}, bf16[4096,4,128]{2,1,0:T(4,128)(2,1)}, u32[]{:S(2)}) copy-start(bf16[4096,4,128]{2,1,0:T(4,128)(2,1)} %param.10) | copy-start | bytes 12582916
  40.8 5.2 %copy-start.2 = (bf16[4096,128]{1,0:T(8,128)(2,1)S(1)}, bf16[4096,128]{1,0:T(8,128)(2,1)}, u32[]{:S(2)}) copy-start(bf16[4096,128]{1,0:T(8,128)(2,1)} %param.11) | copy-start | bytes 3145732
  252.8 6.0 %copy-start.5 = (u32[32]{0:T(128)S(1)}, u32[32]{0:T(128)}, u32[]{:S(2)}) copy-start(u32[32]{0:T(128)} %constant.109) | copy-start | bytes 388
Sparse Core Ops, SparseCore 0:
  259.0 34.3 all-reduce.3
where the time goes:
time: 304 us; the launch traced here: 302 us
  matrix products  163 us (54%)
  local copies, waits for them, and re-layouts  50.4 us (17%)
  waiting for transfers between devices  33.2 us (11%)
  between operations  14.9 us (5%)
  blocking collectives  14.4 us (5%)
  other arithmetic  11.6 us (4%)
  starting transfers between devices  8.49 us (3%)
  loops' own time  5.98 us (2%)
    sub x8, matrix products, window_block(): shifted_exp = jnp.exp(scores - highest)  59.7 us
    dot_general x8, matrix products, window_block(): jnp.einsum('hwk,kd->whd', weights, value_window, preferred_element_type=j...  33.7 us
    unnamed x2, waiting for transfers between devices  33.2 us
    dynamic_update_slice x40, local copies, waits for them, and re-layouts, per_device(): lax.map(one_block, (jnp.arange(block_count, dtype=jnp.int32), starts))  25 us
    dot_general x8, matrix products, window_block(): jnp.einsum('hws,sd->whd', linear_scores, value_block, preferred_element_t...  17.5 us
    dot_general x8, matrix products, window_block(): jnp.einsum('hws,sf->whf', back_scores, key_block, preferred_element_type=...  16.1 us
    all_gather x1, blocking collectives, carried_in(): everything = lax.all_gather(array, axis)  14.4 us
    dot_general x8, matrix products, window_block(): jnp.einsum('whf,fd->whd', feature_block.astype(jnp.float32), start_state,...  13.8 us
  transfers between devices with their start and end apart: 3, of which 1 were waited for; matrix products, arithmetic and copies ran while one was open for 5% of the time, Pallas kernels for 0%

commit v1 on v0

v1 whole, which is shorter than its diff:
```python
import functools

import jax
import jax.numpy as jnp
from jax import lax
from jax.experimental import pallas as pl
from jax.experimental.pallas import tpu as pltpu
from jax.sharding import PartitionSpec as P

W = 512
TILE = 128


def from_behind(value, axis, steps):
    count = lax.axis_size(axis)
    return lax.ppermute(value, axis, [(s, s + steps) for s in range(count - steps)])


def nt(a, b):
    return lax.dot_general(a, b, (((1,), (1,)), ((), ())), preferred_element_type=jnp.float32)


def tn(a, b):
    return lax.dot_general(a, b, (((0,), (0,)), ((), ())), preferred_element_type=jnp.float32)


def nn(a, b):
    return jnp.dot(a, b, preferred_element_type=jnp.float32)


def split_two(x):
    high = x.astype(jnp.bfloat16)
    return high, (x - high.astype(jnp.float32)).astype(jnp.bfloat16)


def main_kernel(
    tokens_here, heads, tiles, rows_sub,
    q_ref, c_ref, k_ref, v_ref, rim_k_ref, rim_v_ref, key_map_ref, maps_ref, prefix_ref,
    soft_ref, linear_ref, grad_ref,
    k_ext, v_ext, kf_all, head_mask, state,
):
    step = pl.program_id(0)
    rank = lax.axis_index("seq")
    hd = q_ref.shape[1]
    rows = TILE * heads

    @pl.when(step == 0)
    def _():
        k_ext[:W] = rim_k_ref[...]
        k_ext[W:] = k_ref[...]
        v_ext[:W, :hd] = rim_v_ref[...]
        v_ext[W:, :hd] = v_ref[...]
        v_ext[:, hd:] = jnp.ones((v_ext.shape[0], hd), jnp.bfloat16)
        kf_all[...] = nn(k_ref[...], key_map_ref[...]).astype(jnp.bfloat16)
        row = lax.broadcasted_iota(jnp.int32, head_mask.shape, 0) % heads
        column = lax.broadcasted_iota(jnp.int32, head_mask.shape, 1) // hd
        head_mask[...] = jnp.where(row == column, 1.0, 0.0).astype(jnp.bfloat16)
        state[...] = prefix_ref[...]
        grad_ref[...] = jnp.zeros_like(grad_ref)

    scale = hd ** (-0.5) * 1.4426950408889634
    zero = jnp.zeros((TILE, hd), jnp.bfloat16)
    mids = W // TILE
    for tile in range(tiles):
        index = step * tiles + tile
        first = pl.multiple_of(index * TILE, TILE)
        k_win = k_ext[pl.ds(first, W + TILE), :]
        v_win = v_ext[pl.ds(first, W + TILE), :]
        kf = kf_all[pl.ds(first, TILE), :]
        v = v_ref[pl.ds(first, TILE), :]
        s_now = state[...]
        s_hi, s_lo = split_two(s_now)
        t_hi, t_lo = split_two(s_now.T)

        def diagonal(a, b):
            return jnp.concatenate(
                [jnp.concatenate([a, zero], 1), jnp.concatenate([zero, b], 1)], 0
            )

        into_scores = diagonal(kf, v)
        from_scores = jnp.concatenate([diagonal(v, kf), diagonal(s_hi, t_hi), diagonal(s_lo, t_lo)], 0)
        invalid = [
            jnp.where((rank == 0) & (index + j < mids), -1e30, 0.0).astype(jnp.float32)
            for j in range(mids)
        ]
        gradients = []
        for sub in range(rows // rows_sub):
            start = tile * rows + sub * rows_sub
            q = q_ref[start : start + rows_sub, :]
            c = c_ref[start : start + rows_sub, :]
            shape = (rows_sub, TILE)
            local = (lax.broadcasted_iota(jnp.int32, shape, 0) + sub * rows_sub) // heads
            ahead = lax.broadcasted_iota(jnp.int32, shape, 1) > local
            scores = nt(q, k_win)
            parts = [scores[:, j * TILE : (j + 1) * TILE] for j in range(mids + 1)]
            parts = [p + invalid[j] if j < mids else p for j, p in enumerate(parts)]
            both = jnp.where(ahead, parts[0], parts[mids])
            kept = [both] + parts[1:mids]
            highest = jnp.max(functools.reduce(jnp.maximum, kept), axis=1, keepdims=True)
            kept = [jnp.exp2((p - highest) * scale) for p in kept]
            weights = jnp.concatenate(
                [jnp.where(ahead, kept[0], 0.0).astype(jnp.bfloat16)]
                + [p.astype(jnp.bfloat16) for p in kept[1:]]
                + [jnp.where(ahead, 0.0, kept[0]).astype(jnp.bfloat16)], 1
            )
            soft = nn(weights, v_win)
            soft_ref[start : start + rows_sub, :] = (soft[:, :hd] / soft[:, hd:]).astype(jnp.bfloat16)
            mask = head_mask[...]
            q_heads = jnp.concatenate([q] * heads, 1) * mask
            qf = nn(q_heads, maps_ref[...]).astype(jnp.bfloat16)
            pair = jnp.concatenate([qf, c], 1)
            pair_scores = nt(pair, into_scores)
            ahead_two = jnp.concatenate([ahead, ahead], 1)
            pair_scores = jnp.where(ahead_two, 0.0, pair_scores).astype(jnp.bfloat16)
            pair_out = nn(jnp.concatenate([pair_scores, pair, pair], 1), from_scores)
            position = rank * tokens_here + index * TILE + local + 1
            factor = lax.rsqrt(position.astype(jnp.float32))
            linear_ref[start : start + rows_sub, :] = (factor * pair_out[:, :hd]).astype(jnp.bfloat16)
            fg = (factor * pair_out[:, hd:]).astype(jnp.bfloat16)
            gradients.append(jnp.concatenate([fg] * heads, 1) * mask)
        grad_ref[...] += tn(
            q_ref[tile * rows : (tile + 1) * rows, :], jnp.concatenate(gradients, 0)
        )
        state[...] = s_now + tn(kf, v)


def per_device(queries, keys, values, query_maps, key_map, linear_cotangent):
    tokens_here, head_dim = keys.shape
    heads = queries.shape[1]
    count = lax.axis_size("seq")
    rank = lax.axis_index("seq")
    rim_keys, rim_values = from_behind(
        (keys[tokens_here - W :], values[tokens_here - W :]), "seq", 1
    )
    key_features = jnp.dot(keys, key_map, preferred_element_type=jnp.float32).astype(jnp.bfloat16)
    local_sum = lax.dot_general(
        key_features, values, (((0,), (0,)), ((), ())), preferred_element_type=jnp.float32
    )
    prefix = jnp.zeros_like(local_sum)
    for k in range(1, count):
        prefix = prefix + from_behind(local_sum, "seq", k)

    tiles = 4
    rows_sub = min(256, TILE * heads)
    step_rows = TILE * tiles * heads
    total = tokens_here * heads
    whole = lambda a: pl.BlockSpec(a.shape, lambda i: (0,) * a.ndim)
    rows_spec = pl.BlockSpec((step_rows, head_dim), lambda i: (i, 0))
    maps = query_maps.reshape(heads * head_dim, head_dim)
    soft, linear, grad = pl.pallas_call(
        functools.partial(main_kernel, tokens_here, heads, tiles, rows_sub),
        grid=(total // step_rows,),
        in_specs=[rows_spec, rows_spec]
        + [whole(a) for a in (keys, values, rim_keys, rim_values, key_map, maps, prefix)],
        out_specs=[rows_spec, rows_spec, pl.BlockSpec((head_dim, heads * head_dim), lambda i: (0, 0))],
        out_shape=[
            jax.ShapeDtypeStruct((total, head_dim), jnp.bfloat16),
            jax.ShapeDtypeStruct((total, head_dim), jnp.bfloat16),
            jax.ShapeDtypeStruct((head_dim, heads * head_dim), jnp.float32),
        ],
        scratch_shapes=[
            pltpu.VMEM((tokens_here + W, head_dim), jnp.bfloat16),
            pltpu.VMEM((tokens_here + W, 2 * head_dim), jnp.bfloat16),
            pltpu.VMEM((tokens_here, head_dim), jnp.bfloat16),
            pltpu.VMEM((rows_sub, heads * head_dim), jnp.bfloat16),
            pltpu.VMEM((head_dim, head_dim), jnp.float32),
        ],
        compiler_params=pltpu.CompilerParams(dimension_semantics=("arbitrary",)),
        name="attention",
    )(
        queries.reshape(total, head_dim), linear_cotangent.reshape(total, head_dim),
        keys, values, rim_keys, rim_values, key_map, maps, prefix,
    )
    share = head_dim // count
    piece = lambda k: lax.dynamic_slice_in_dim(grad, ((rank + k) % count) * share, share, 0)
    mine = piece(0)
    for k in range(1, count):
        mine = mine + lax.ppermute(piece(k), "seq", [(s, (s + k) % count) for s in range(count)])
    shape = (tokens_here, heads, head_dim)
    return soft.reshape(shape), linear.reshape(shape), mine.reshape(share, heads, head_dim)


def solution(mesh):
    rows = P(("groups", "seq"), ("head", "rep"), None)
    return jax.shard_map(
        per_device,
        mesh=mesh,
        in_specs=(
            rows,
            P(("groups", "seq"), None),
            P(("groups", "seq"), None),
            P(("groups", "head", "rep"), None, None),
            P("groups", None),
            rows,
        ),
        out_specs=(rows, rows, rows),
        check_vma=False,
    )
```

time: 304 us -> 87.9 us (0.29)
  matrix products: 163 us -> 2.43 us
  Pallas kernels: 0 us -> 52.5 us
  local copies, waits for them, and re-layouts: 50.4 us -> 4.05 us
  waiting for transfers between devices: 33.2 us -> 7.17 us
  blocking collectives: 14.4 us -> 0 us
  between operations: 14.9 us -> 0.77 us
  starting transfers between devices: 8.49 us -> 19.1 us
  other arithmetic: 11.6 us -> 1.5 us
  loops' own time: 5.98 us -> 0 us
    dot_general x44 -> x1, matrix products: 103 us -> 2.43 us  [per_device(): lax.dot_general(key_features, values, (((0,), (0,)), ((), ())), preferred...]
    sub x8 -> x0, matrix products: 59.7 us -> none  [window_block(): shifted_exp = jnp.exp(scores - highest)]
    pallas_call x0 -> x1, Pallas kernels: none -> 52.5 us  [per_device(): pl.pallas_call(functools.partial(main_kernel, tokens_here, heads, tiles,...]
    unnamed x2 -> x0, waiting for transfers between devices: 33.2 us -> none
    dynamic_update_slice x40 -> x0, local copies, waits for them, and re-layouts: 25 us -> none  [per_device(): lax.map(one_block, (jnp.arange(block_count, dtype=jnp.int32), starts))]
    all_gather x1 -> x0, blocking collectives: 14.4 us -> none  [carried_in(): everything = lax.all_gather(array, axis)]
    dynamic_slice x16 -> x1, local copies, waits for them, and re-layouts: 14.7 us -> 0.93 us  [per_device(): lax.dynamic_slice_in_dim(grad, (rank + k) % count * share, share, 0)]
    ppermute x2 -> x8, starting transfers between devices: 8.45 us -> 19.1 us  [the longest x5 14.5 us: from_behind(): lax.ppermute(value, axis, [(s, s + steps) for s in range(count - steps)])]
  transfers between devices with their start and end apart: 3 -> 8, of which waited for: 1 -> 4; matrix products, arithmetic and copies ran while one was open for 5% -> 3% of each run, Pallas kernels for 0% -> 0%
where the time goes in v1:
time: 87.9 us; the launch traced here: 87.5 us
  Pallas kernels  52.5 us (60%)
  starting transfers between devices  19.1 us (22%)
  waiting for transfers between devices  7.17 us (8%)
  local copies, waits for them, and re-layouts  4.05 us (5%)
  matrix products  2.43 us (3%)
  other arithmetic  1.5 us (2%)
    pallas_call x1, Pallas kernels, per_device(): pl.pallas_call(functools.partial(main_kernel, tokens_here, heads, tiles,...  52.5 us
    ppermute x5, starting transfers between devices, from_behind(): lax.ppermute(value, axis, [(s, s + steps) for s in range(count - steps)])  14.5 us
    ppermute x3, waiting for transfers between devices, per_device(): lax.ppermute(piece(k), 'seq', [(s, (s + k) % count) for s in range(count)])  5.39 us
    ppermute x3, starting transfers between devices, per_device(): lax.ppermute(piece(k), 'seq', [(s, (s + k) % count) for s in range(count)])  4.63 us
    dot_general x1, matrix products, per_device(): lax.dot_general(key_features, values, (((0,), (0,)), ((), ())), preferred...  2.43 us
    ppermute x5, waiting for transfers between devices, from_behind(): lax.ppermute(value, axis, [(s, s + steps) for s in range(count - steps)])  1.78 us
  transfers between devices with their start and end apart: 8, of which 4 were waited for; matrix products, arithmetic and copies ran while one was open for 3% of the time, Pallas kernels for 0%

profile of v1, /device:TPU:0, one launch (start us, length us, event | category | flops | bytes accessed | tf_op | source)
XLA Modules:
  0.0 87.5 jit_solution(10189407787057052638)
XLA Ops:
  0.6 2.4 %fusion = f32[128,128]{1,0:T(8,128)S(1)} fusion(bf16[4096,128]{1,0:T(8,128)(2,1)} %v_ref.1, bf16[4096,128]{1,0:T(8,128)(2,1)} %k_ref.1, bf16[128,128]{1,0:T(8,128)(2,1)} %key_map_ref.1), kind=kOutput, calls=%fused_computation.1 | convolution fusion | flops 268959744 | bytes 2195456 | tf_op jit(solution)/shard_map/dot_general | solution.py:136
  3.1 7.0 %collective-permute-start.4 = (f32[128,128]{1,0:T(8,128)S(1)}, f32[128,128]{1,0:T(8,128)S(1)}, u32[]{:S(2)}, u32[]{:S(2)}) collective-permute-start(f32[128,128]{1,0:T(8,128)S(1)} %fusion), channel_id=1, source_target_pairs={{0,12},{1,13},{2,14},{3,15},{16,28},{17,29},{18,30},{19,31}} | collective-permute-start | bytes 196616 | tf_op jit(solution)/shard_map/ppermute | solution.py:16
  10.1 1.3 %collective-permute-start.2 = (f32[128,128]{1,0:T(8,128)S(1)}, f32[128,128]{1,0:T(8,128)S(1)}, u32[]{:S(2)}, u32[]{:S(2)}) collective-permute-start(f32[128,128]{1,0:T(8,128)S(1)} %fusion), channel_id=1, source_target_pairs={{0,4},{4,8},{8,12},{1,5},{5,9},{9,13},{2,6},{6,10},{10,14},{3,7},{... | collective-permute-start | bytes 196616 | tf_op jit(solution)/shard_map/ppermute | solution.py:16
  11.4 2.5 %collective-permute-start.3 = (f32[128,128]{1,0:T(8,128)S(1)}, f32[128,128]{1,0:T(8,128)S(1)}, u32[]{:S(2)}, u32[]{:S(2)}) collective-permute-start(f32[128,128]{1,0:T(8,128)S(1)} %fusion), channel_id=1, source_target_pairs={{0,8},{4,12},{1,9},{5,13},{2,10},{6,14},{3,11},{7,15},{16,24},{20,... | collective-permute-start | bytes 196616 | tf_op jit(solution)/shard_map/ppermute | solution.py:16
  13.8 0.9 %slice.6 = bf16[512,128]{1,0:T(8,128)(2,1)S(1)} slice(bf16[4096,128]{1,0:T(8,128)(2,1)} %k_ref.1), slice={[3584:4096], [0:128]} | slice | bytes 262144 | tf_op jit(solution)/shard_map/slice | solution.py:133
  14.8 1.3 %collective-permute-start = (bf16[512,128]{1,0:T(8,128)(2,1)S(1)}, bf16[512,128]{1,0:T(8,128)(2,1)S(1)}, u32[]{:S(2)}, u32[]{:S(2)}) collective-permute-start(bf16[512,128]{1,0:T(8,128)(2,1)S(1)} %slice.6), channel_id=1, source_target_pairs={{0,4},{4,8},{8,12},{1,5},{5,9},{9,13},{2,6},{6,10},{10,14},{3,7},{... | collective-permute-start | bytes 393224 | tf_op jit(solution)/shard_map/ppermute | solution.py:16
  16.1 0.9 %slice.7 = bf16[512,128]{1,0:T(8,128)(2,1)S(1)} slice(bf16[4096,128]{1,0:T(8,128)(2,1)} %v_ref.1), slice={[3584:4096], [0:128]} | slice | bytes 262144 | tf_op jit(solution)/shard_map/slice | solution.py:133
  17.0 2.5 %collective-permute-start.1 = (bf16[512,128]{1,0:T(8,128)(2,1)S(1)}, bf16[512,128]{1,0:T(8,128)(2,1)S(1)}, u32[]{:S(2)}, u32[]{:S(2)}) collective-permute-start(bf16[512,128]{1,0:T(8,128)(2,1)S(1)} %slice.7), channel_id=1, source_target_pairs={{0,4},{4,8},{8,12},{1,5},{5,9},{9,13},{2,6},{6,10},{10,14},{3,7},{... | collective-permute-start | bytes 393224 | tf_op jit(solution)/shard_map/ppermute | solution.py:16
  19.5 0.0 collective-permute-done.4
  19.5 0.0 collective-permute-done.2
  19.5 0.0 collective-permute-done.3
  19.5 0.6 add_add_fusion.1.prefix_ref
  20.2 1.8 %collective-permute-done.1.rim_v_ref = bf16[512,128]{1,0:T(8,128)(2,1)S(1)} collective-permute-done((bf16[512,128]{1,0:T(8,128)(2,1)S(1)}, bf16[512,128]{1,0:T(8,128)(2,1)S(1)}, u32[]{:S(2)}, u32[]{:S(2)}) %collective-permute-start.1) | collective-permute-done | bytes 131104 | tf_op jit(solution)/shard_map/ppermute | solution.py:16
  22.0 0.6 copy-done.1
  22.6 52.5 %attention.1 = (bf16[16384,128]{1,0:T(8,128)(2,1)}, bf16[16384,128]{1,0:T(8,128)(2,1)}, f32[128,512]{1,0:T(8,128)}) custom-call(bf16[16384,128]{1,0:T(8,128)(2,1)} %bitcast.8, bf16[16384,128]{1,0:T(8,128)(2,1)} %bitcast.9, bf16[4096,128]{1,0:T(8,128)(2,1)} %k_ref.1, bf16[4096,128]{1,0:T(8,128)(2,1)} %v_ref.1, bf16[512,128]{1,0:T(8,128)(2,1)} %copy-done, ...), custom_call_target="tpu_custom_call" | custom-call | tf_op jit(solution)/shard_map/attention/pallas_call | solution.py:150
  75.1 0.9 %constant_dynamic-slice_fusion.2 = (f32[32,512]{1,0:T(8,128)S(1)}, f32[32,512]{1,0:T(8,128)S(1)}, f32[32,512]{1,0:T(8,128)S(1)}) fusion(f32[128,512]{1,0:T(8,128)} %get-tuple-element.8, s32[]{:T(128)S(6)} %select_n.34, s32[]{:T(128)S(6)} %select_n.38, s32[]{:T(128)S(6)} %select_n.36), kind=kLoop, calls=%fused_computation.6 | loop fusion | bytes 393228 | tf_op jit(solution)/shard_map/dynamic_slice | solution.py:175
  76.0 1.7 %collective-permute-start.7 = (f32[32,512]{1,0:T(8,128)S(1)}, f32[32,512]{1,0:T(8,128)S(1)}, u32[]{:S(2)}, u32[]{:S(2)}) collective-permute-start(f32[32,512]{1,0:T(8,128)S(1)} %get-tuple-element.10), channel_id=1, source_target_pairs={{0,12},{4,0},{8,4},{12,8},{1,13},{5,1},{9,5},{13,9},{2,14},{6,2},{... | collective-permute-start | bytes 196616 | tf_op jit(solution)/shard_map/ppermute | solution.py:178
  77.7 2.3 %collective-permute-start.6 = (f32[32,512]{1,0:T(8,128)S(1)}, f32[32,512]{1,0:T(8,128)S(1)}, u32[]{:S(2)}, u32[]{:S(2)}) collective-permute-start(f32[32,512]{1,0:T(8,128)S(1)} %get-tuple-element.11), channel_id=1, source_target_pairs={{0,8},{4,12},{8,0},{12,4},{1,9},{5,13},{9,1},{13,5},{2,10},{6,14},... | collective-permute-start | bytes 196616 | tf_op jit(solution)/shard_map/ppermute | solution.py:178
  80.0 0.7 collective-permute-start.5
  80.6 0.7 collective-permute-done.7
  81.3 3.0 %collective-permute-done.6 = f32[32,512]{1,0:T(8,128)S(1)} collective-permute-done((f32[32,512]{1,0:T(8,128)S(1)}, f32[32,512]{1,0:T(8,128)S(1)}, u32[]{:S(2)}, u32[]{:S(2)}) %collective-permute-start.6) | collective-permute-done | bytes 65568 | tf_op jit(solution)/shard_map/ppermute | solution.py:178
  84.3 1.7 %collective-permute-done.5 = f32[32,512]{1,0:T(8,128)S(1)} collective-permute-done((f32[32,512]{1,0:T(8,128)S(1)}, f32[32,512]{1,0:T(8,128)S(1)}, u32[]{:S(2)}, u32[]{:S(2)}) %collective-permute-start.5) | collective-permute-done | bytes 65568 | tf_op jit(solution)/shard_map/ppermute | solution.py:178
  86.0 0.9 add_add_fusion
  86.9 0.7 reshape.29
  (4 shorter events, 0.0 us)
Async XLA Ops:
  3.1 16.4 %collective-permute-start.4 = (f32[128,128]{1,0:T(8,128)S(1)}, f32[128,128]{1,0:T(8,128)S(1)}, u32[]{:S(2)}, u32[]{:S(2)}) collective-permute-start(f32[128,128]{1,0:T(8,128)S(1)} %fusion), channel_id=1, source_target_pairs={{0,12},{1,13},{2,14},{3,15},{16,28},{17,29},{18,30},{19,31}} | collective-permute-start | bytes 196616 | tf_op jit(solution)/shard_map/ppermute | solution.py:16
  10.1 9.5 %collective-permute-start.2 = (f32[128,128]{1,0:T(8,128)S(1)}, f32[128,128]{1,0:T(8,128)S(1)}, u32[]{:S(2)}, u32[]{:S(2)}) collective-permute-start(f32[128,128]{1,0:T(8,128)S(1)} %fusion), channel_id=1, source_target_pairs={{0,4},{4,8},{8,12},{1,5},{5,9},{9,13},{2,6},{6,10},{10,14},{3,7},{... | collective-permute-start | bytes 196616 | tf_op jit(solution)/shard_map/ppermute | solution.py:16
  11.4 8.2 %collective-permute-start.3 = (f32[128,128]{1,0:T(8,128)S(1)}, f32[128,128]{1,0:T(8,128)S(1)}, u32[]{:S(2)}, u32[]{:S(2)}) collective-permute-start(f32[128,128]{1,0:T(8,128)S(1)} %fusion), channel_id=1, source_target_pairs={{0,8},{4,12},{1,9},{5,13},{2,10},{6,14},{3,11},{7,15},{16,24},{20,... | collective-permute-start | bytes 196616 | tf_op jit(solution)/shard_map/ppermute | solution.py:16
  14.8 5.4 %collective-permute-start = (bf16[512,128]{1,0:T(8,128)(2,1)S(1)}, bf16[512,128]{1,0:T(8,128)(2,1)S(1)}, u32[]{:S(2)}, u32[]{:S(2)}) collective-permute-start(bf16[512,128]{1,0:T(8,128)(2,1)S(1)} %slice.6), channel_id=1, source_target_pairs={{0,4},{4,8},{8,12},{1,5},{5,9},{9,13},{2,6},{6,10},{10,14},{3,7},{... | collective-permute-start | bytes 393224 | tf_op jit(solution)/shard_map/ppermute | solution.py:16
  17.0 5.0 %collective-permute-start.1 = (bf16[512,128]{1,0:T(8,128)(2,1)S(1)}, bf16[512,128]{1,0:T(8,128)(2,1)S(1)}, u32[]{:S(2)}, u32[]{:S(2)}) collective-permute-start(bf16[512,128]{1,0:T(8,128)(2,1)S(1)} %slice.7), channel_id=1, source_target_pairs={{0,4},{4,8},{8,12},{1,5},{5,9},{9,13},{2,6},{6,10},{10,14},{3,7},{... | collective-permute-start | bytes 393224 | tf_op jit(solution)/shard_map/ppermute | solution.py:16
  20.2 1.8 %copy-start = (bf16[512,128]{1,0:T(8,128)(2,1)}, bf16[512,128]{1,0:T(8,128)(2,1)S(1)}, u32[]{:S(2)}) copy-start(bf16[512,128]{1,0:T(8,128)(2,1)S(1)} %collective-permute-done.rim_k_ref) | copy-start | bytes 393220
  22.0 0.6 copy-start.1
  76.0 5.3 %collective-permute-start.7 = (f32[32,512]{1,0:T(8,128)S(1)}, f32[32,512]{1,0:T(8,128)S(1)}, u32[]{:S(2)}, u32[]{:S(2)}) collective-permute-start(f32[32,512]{1,0:T(8,128)S(1)} %get-tuple-element.10), channel_id=1, source_target_pairs={{0,12},{4,0},{8,4},{12,8},{1,13},{5,1},{9,5},{13,9},{2,14},{6,2},{... | collective-permute-start | bytes 196616 | tf_op jit(solution)/shard_map/ppermute | solution.py:178
  77.7 6.6 %collective-permute-start.6 = (f32[32,512]{1,0:T(8,128)S(1)}, f32[32,512]{1,0:T(8,128)S(1)}, u32[]{:S(2)}, u32[]{:S(2)}) collective-permute-start(f32[32,512]{1,0:T(8,128)S(1)} %get-tuple-element.11), channel_id=1, source_target_pairs={{0,8},{4,12},{8,0},{12,4},{1,9},{5,13},{9,1},{13,5},{2,10},{6,14},... | collective-permute-start | bytes 196616 | tf_op jit(solution)/shard_map/ppermute | solution.py:178
  80.0 6.1 %collective-permute-start.5 = (f32[32,512]{1,0:T(8,128)S(1)}, f32[32,512]{1,0:T(8,128)S(1)}, u32[]{:S(2)}, u32[]{:S(2)}) collective-permute-start(f32[32,512]{1,0:T(8,128)S(1)} %get-tuple-element.9), channel_id=1, source_target_pairs={{0,4},{4,8},{8,12},{12,0},{1,5},{5,9},{9,13},{13,1},{2,6},{6,10},{... | collective-permute-start | bytes 196616 | tf_op jit(solution)/shard_map/ppermute | solution.py:178

commit v2 on v1

v2 whole, which is shorter than its diff:
```python
import functools

import jax
import jax.numpy as jnp
from jax import lax
from jax.experimental import pallas as pl
from jax.experimental.pallas import tpu as pltpu
from jax.sharding import PartitionSpec as P

W = 512
TILE = 128
MESH = pl.DeviceIdType.MESH


def nt(a, b):
    return lax.dot_general(a, b, (((1,), (1,)), ((), ())), preferred_element_type=jnp.float32)


def tn(a, b):
    return lax.dot_general(a, b, (((0,), (0,)), ((), ())), preferred_element_type=jnp.float32)


def nn(a, b):
    return jnp.dot(a, b, preferred_element_type=jnp.float32)


def split_two(x):
    high = x.astype(jnp.bfloat16)
    return high, (x - high.astype(jnp.float32)).astype(jnp.bfloat16)


def head_masks(rows, heads, inner, hd):
    def mask(parts, of_head):
        shape = (rows, parts * hd)
        head = lax.broadcasted_iota(jnp.int32, shape, 0) % heads
        part = lax.broadcasted_iota(jnp.int32, shape, 1) // hd
        return jnp.where(of_head(head) == part, 1.0, 0.0).astype(jnp.bfloat16)

    return mask(heads // inner, lambda h: h // inner), mask(inner, lambda h: h % inner)


def seq_barrier(rank, count):
    barrier = pltpu.get_barrier_semaphore()
    for k in range(1, count):
        pl.semaphore_signal(
            barrier, inc=1, device_id={"seq": lax.rem(rank + k, count)}, device_id_type=MESH
        )
    return barrier


def first_kernel(
    count, heads, inner, steps,
    q_ref, maps_ref, k_ref, v_ref, key_map_ref,
    qf_ref, kf_ref, rim_k_ref, rim_v_ref, prefix_ref,
    outer_mask, local_sum, sums, halo, sum_send, sum_recv, halo_send, halo_recv,
):
    step = pl.program_id(0)
    rank = lax.axis_index("seq")
    tokens, hd = k_ref.shape
    rows = outer_mask.shape[0]

    def halo_copy(i):
        return pltpu.make_async_remote_copy(
            src_ref=(k_ref, v_ref)[i].at[pl.ds(tokens - W, W)],
            dst_ref=halo.at[i],
            send_sem=halo_send.at[i],
            recv_sem=halo_recv.at[i],
            device_id={"seq": rank + 1},
            device_id_type=MESH,
        )

    def sum_copy(k):
        return pltpu.make_async_remote_copy(
            src_ref=local_sum,
            dst_ref=sums.at[k - 1],
            send_sem=sum_send.at[k - 1],
            recv_sem=sum_recv.at[k - 1],
            device_id={"seq": rank + k},
            device_id_type=MESH,
        )

    @pl.when(step == 0)
    def _():
        barrier = seq_barrier(rank, count)
        kf_ref[...] = nn(k_ref[...], key_map_ref[...]).astype(jnp.bfloat16)
        local_sum[...] = tn(kf_ref[...], v_ref[...])
        outer_mask[...] = head_masks(rows, heads, inner, hd)[0]
        pl.semaphore_wait(barrier, count - 1)
        for k in range(1, count):
            @pl.when(rank + k < count)
            def _():
                sum_copy(k).start()
        @pl.when(rank + 1 < count)
        def _():
            halo_copy(0).start()
            halo_copy(1).start()

    outer = heads // inner
    maps = jnp.concatenate(
        [
            jnp.concatenate([maps_ref[(a * inner + b) * hd : (a * inner + b + 1) * hd] for b in range(inner)], 1)
            for a in range(outer)
        ], 0
    )
    inner_head = lax.broadcasted_iota(jnp.int32, (rows, hd), 0) % inner
    for start in range(0, q_ref.shape[0], rows):
        q = q_ref[start : start + rows, :]
        spread = nn(jnp.concatenate([q] * outer, 1) * outer_mask[...], maps)
        qf = spread[:, :hd]
        for b in range(1, inner):
            qf = jnp.where(inner_head == b, spread[:, b * hd : (b + 1) * hd], qf)
        qf_ref[start : start + rows, :] = qf.astype(jnp.bfloat16)

    @pl.when(step == steps - 1)
    def _():
        prefix_ref[...] = jnp.zeros_like(prefix_ref)
        for k in range(1, count):
            @pl.when(rank + k < count)
            def _():
                sum_copy(k).wait_send()
            @pl.when(rank >= k)
            def _():
                sum_copy(k).wait_recv()
                prefix_ref[...] += sums[k - 1]
        @pl.when(rank + 1 < count)
        def _():
            halo_copy(0).wait_send()
            halo_copy(1).wait_send()
        @pl.when(rank >= 1)
        def _():
            halo_copy(0).wait_recv()
            halo_copy(1).wait_recv()
            rim_k_ref[...] = halo[0]
            rim_v_ref[...] = halo[1]
        @pl.when(rank == 0)
        def _():
            rim_k_ref[...] = jnp.zeros_like(rim_k_ref)
            rim_v_ref[...] = jnp.zeros_like(rim_v_ref)


def last_kernel(count, g_ref, g16_ref, out_ref, slots, send_sem, recv_sem):
    rank = lax.axis_index("seq")
    barrier = seq_barrier(rank, count)
    pl.semaphore_wait(barrier, count - 1)
    copies = []
    for k in range(1, count):
        target = lax.rem(rank + k, count)
        copies.append(pltpu.make_async_remote_copy(
            src_ref=g16_ref.at[target],
            dst_ref=slots.at[k - 1],
            send_sem=send_sem.at[k - 1],
            recv_sem=recv_sem.at[k - 1],
            device_id={"seq": target},
            device_id_type=MESH,
        ))
    for copy in copies:
        copy.start()
    total = g_ref[rank]
    for k, copy in enumerate(copies):
        copy.wait()
        total = total + slots[k].astype(jnp.float32)
    out_ref[...] = total


def main_kernel(
    tokens_here, heads, inner, tiles, rows_sub, steps,
    q_ref, qf_ref, c_ref, k_ref, v_ref, kf_ref, rim_k_ref, rim_v_ref, prefix_ref,
    soft_ref, linear_ref, grad_ref, grad16_ref,
    k_ext, v_ext, outer_mask, inner_mask, state, grad,
):
    step = pl.program_id(0)
    rank = lax.axis_index("seq")
    hd = q_ref.shape[1]
    rows = TILE * heads
    outer = heads // inner

    @pl.when(step == 0)
    def _():
        k_ext[:W] = rim_k_ref[...]
        k_ext[W:] = k_ref[...]
        v_ext[:W, :hd] = rim_v_ref[...]
        v_ext[W:, :hd] = v_ref[...]
        v_ext[:, hd:] = jnp.ones((v_ext.shape[0], hd), jnp.bfloat16)
        outer_mask[...], inner_mask[...] = head_masks(rows_sub, heads, inner, hd)
        state[...] = prefix_ref[...]
        grad[...] = jnp.zeros_like(grad)

    scale = hd ** (-0.5) * 1.4426950408889634
    zero = jnp.zeros((TILE, hd), jnp.bfloat16)
    mids = W // TILE
    for tile in range(tiles):
        index = step * tiles + tile
        first = pl.multiple_of(index * TILE, TILE)
        k_win = k_ext[pl.ds(first, W + TILE), :]
        v_win = v_ext[pl.ds(first, W + TILE), :]
        kf = kf_ref[pl.ds(first, TILE), :]
        v = v_ref[pl.ds(first, TILE), :]
        s_now = state[...]
        s_hi, s_lo = split_two(s_now)
        t_hi, t_lo = split_two(s_now.T)

        def diagonal(a, b):
            return jnp.concatenate(
                [jnp.concatenate([a, zero], 1), jnp.concatenate([zero, b], 1)], 0
            )

        into_scores = diagonal(kf, v)
        from_scores = jnp.concatenate([diagonal(v, kf), diagonal(s_hi, t_hi), diagonal(s_lo, t_lo)], 0)
        invalid = [
            jnp.where((rank == 0) & (index + j < mids), -1e30, 0.0).astype(jnp.float32)
            for j in range(mids)
        ]
        queries, gradients = [], []
        for sub in range(rows // rows_sub):
            start = tile * rows + sub * rows_sub
            q = q_ref[start : start + rows_sub, :]
            c = c_ref[start : start + rows_sub, :]
            shape = (rows_sub, TILE)
            local = (lax.broadcasted_iota(jnp.int32, shape, 0) + sub * rows_sub) // heads
            ahead = lax.broadcasted_iota(jnp.int32, shape, 1) > local
            scores = nt(q, k_win)
            parts = [scores[:, j * TILE : (j + 1) * TILE] for j in range(mids + 1)]
            parts = [p + invalid[j] if j < mids else p for j, p in enumerate(parts)]
            both = jnp.where(ahead, parts[0], parts[mids])
            kept = [both] + parts[1:mids]
            highest = jnp.max(functools.reduce(jnp.maximum, kept), axis=1, keepdims=True)
            kept = [jnp.exp2((p - highest) * scale) for p in kept]
            weights = jnp.concatenate(
                [jnp.where(ahead, kept[0], 0.0).astype(jnp.bfloat16)]
                + [p.astype(jnp.bfloat16) for p in kept[1:]]
                + [jnp.where(ahead, 0.0, kept[0]).astype(jnp.bfloat16)], 1
            )
            soft = nn(weights, v_win)
            soft_ref[start : start + rows_sub, :] = (soft[:, :hd] / soft[:, hd:]).astype(jnp.bfloat16)
            pair = jnp.concatenate([qf_ref[start : start + rows_sub, :], c], 1)
            pair_scores = nt(pair, into_scores)
            ahead_two = jnp.concatenate([ahead, ahead], 1)
            pair_scores = jnp.where(ahead_two, 0.0, pair_scores).astype(jnp.bfloat16)
            pair_out = nn(jnp.concatenate([pair_scores, pair, pair], 1), from_scores)
            position = rank * tokens_here + index * TILE + local + 1
            factor = lax.rsqrt(position.astype(jnp.float32))
            linear_ref[start : start + rows_sub, :] = (factor * pair_out[:, :hd]).astype(jnp.bfloat16)
            fg = (factor * pair_out[:, hd:]).astype(jnp.bfloat16)
            queries.append(jnp.concatenate([q] * outer, 1) * outer_mask[...])
            gradients.append(jnp.concatenate([fg] * inner, 1) * inner_mask[...])
        grad[...] += tn(jnp.concatenate(queries, 0), jnp.concatenate(gradients, 0))
        state[...] = s_now + tn(kf, v)

    @pl.when(step == steps - 1)
    def _():
        for a in range(outer):
            block = grad[a * hd : (a + 1) * hd, :]
            block = block.reshape(grad_ref.shape[:2] + (inner * hd,))
            grad_ref[:, :, a * inner * hd : (a + 1) * inner * hd] = block
            grad16_ref[:, :, a * inner * hd : (a + 1) * inner * hd] = block.astype(jnp.bfloat16)


def per_device(queries, keys, values, query_maps, key_map, linear_cotangent):
    tokens_here, hd = keys.shape
    heads = queries.shape[1]
    count = lax.axis_size("seq")
    inner = 2 if heads % 2 == 0 else 1
    outer = heads // inner
    share = hd // count
    tiles = 4
    rows_sub = min(256, TILE * heads)
    step_rows = TILE * tiles * heads
    total = tokens_here * heads
    steps = total // step_rows
    whole = lambda a: pl.BlockSpec(a.shape, lambda i: (0,) * len(a.shape))
    rows_spec = pl.BlockSpec((step_rows, hd), lambda i: (i, 0))
    maps = query_maps.reshape(heads * hd, hd)
    queries = queries.reshape(total, hd)
    cotangent = linear_cotangent.reshape(total, hd)

    rows16 = jax.ShapeDtypeStruct((total, hd), jnp.bfloat16)
    kf16 = jax.ShapeDtypeStruct((tokens_here, hd), jnp.bfloat16)
    rim = jax.ShapeDtypeStruct((W, hd), jnp.bfloat16)
    square = jax.ShapeDtypeStruct((hd, hd), jnp.float32)
    dma = pltpu.SemaphoreType.DMA
    query_features, key_features, rim_keys, rim_values, prefix = pl.pallas_call(
        functools.partial(first_kernel, count, heads, inner, steps),
        grid=(steps,),
        in_specs=[rows_spec] + [whole(a) for a in (maps, keys, values, key_map)],
        out_specs=[rows_spec] + [whole(a) for a in (kf16, rim, rim, square)],
        out_shape=[rows16, kf16, rim, rim, square],
        scratch_shapes=[
            pltpu.VMEM((rows_sub, outer * hd), jnp.bfloat16),
            pltpu.VMEM((hd, hd), jnp.float32),
            pltpu.VMEM((count - 1, hd, hd), jnp.float32),
            pltpu.VMEM((2, W, hd), jnp.bfloat16),
            dma((count - 1,)), dma((count - 1,)), dma((2,)), dma((2,)),
        ],
        compiler_params=pltpu.CompilerParams(
            dimension_semantics=("arbitrary",), collective_id=0, has_side_effects=True
        ),
        name="features",
    )(queries, maps, keys, values, key_map)

    pieces = (count, share, heads * hd)
    small = (keys, values, key_features, rim_keys, rim_values, prefix)
    soft, linear, grad, grad16 = pl.pallas_call(
        functools.partial(main_kernel, tokens_here, heads, inner, tiles, rows_sub, steps),
        grid=(steps,),
        in_specs=[rows_spec] * 3 + [whole(a) for a in small],
        out_specs=[rows_spec] * 2 + [pl.BlockSpec(pieces, lambda i: (0, 0, 0))] * 2,
        out_shape=[
            rows16, rows16,
            jax.ShapeDtypeStruct(pieces, jnp.float32),
            jax.ShapeDtypeStruct(pieces, jnp.bfloat16),
        ],
        scratch_shapes=[
            pltpu.VMEM((tokens_here + W, hd), jnp.bfloat16),
            pltpu.VMEM((tokens_here + W, 2 * hd), jnp.bfloat16),
            pltpu.VMEM((rows_sub, outer * hd), jnp.bfloat16),
            pltpu.VMEM((rows_sub, inner * hd), jnp.bfloat16),
            pltpu.VMEM((hd, hd), jnp.float32),
            pltpu.VMEM((outer * hd, inner * hd), jnp.float32),
        ],
        compiler_params=pltpu.CompilerParams(dimension_semantics=("arbitrary",)),
        name="attention",
    )(queries, query_features, cotangent, *small)

    vmem = pl.BlockSpec(memory_space=pltpu.VMEM)
    mine = pl.pallas_call(
        functools.partial(last_kernel, count),
        in_specs=[vmem, vmem],
        out_specs=vmem,
        out_shape=jax.ShapeDtypeStruct(pieces[1:], jnp.float32),
        scratch_shapes=[
            pltpu.VMEM((count - 1,) + pieces[1:], jnp.bfloat16), dma((count - 1,)), dma((count - 1,)),
        ],
        compiler_params=pltpu.CompilerParams(collective_id=1, has_side_effects=True),
        name="map_gradient",
    )(grad, grad16)
    shape = (tokens_here, heads, hd)
    return soft.reshape(shape), linear.reshape(shape), mine.reshape(share, heads, hd)


def solution(mesh):
    rows = P(("groups", "seq"), ("head", "rep"), None)
    return jax.shard_map(
        per_device,
        mesh=mesh,
        in_specs=(
            rows,
            P(("groups", "seq"), None),
            P(("groups", "seq"), None),
            P(("groups", "head", "rep"), None, None),
            P("groups", None),
            rows,
        ),
        out_specs=(rows, rows, rows),
        check_vma=False,
    )
```

time: 87.9 us -> 71.9 us (0.82)
  starting transfers between devices: 19.1 us -> 0 us
  Pallas kernels: 52.5 us -> 69.4 us
  waiting for transfers between devices: 7.17 us -> 0 us
  local copies, waits for them, and re-layouts: 4.05 us -> 1.49 us
  matrix products: 2.43 us -> 0 us
  other arithmetic: 1.5 us -> 0 us
    ppermute x8 -> x0, starting transfers between devices: 19.1 us -> none  [the longest x5 14.5 us: from_behind(): lax.ppermute(value, axis, [(s, s + steps) for s in range(count - steps)])]
    pallas_call x1 -> x3, Pallas kernels: 52.5 us -> 69.4 us  [the longest x1 42.4 us: per_device(): pl.pallas_call(functools.partial(main_kernel, tokens_here, heads, inner,...]
    ppermute x8 -> x0, waiting for transfers between devices: 7.17 us -> none  [the longest x3 5.39 us: per_device(): lax.ppermute(piece(k), 'seq', [(s, (s + k) % count) for s in range(count)])]
    dot_general x1 -> x0, matrix products: 2.43 us -> none  [per_device(): lax.dot_general(key_features, values, (((0,), (0,)), ((), ())), preferred...]
    slice x2 -> x0, local copies, waits for them, and re-layouts: 1.83 us -> none  [the longest x1 0.92 us: per_device(): keys[tokens_here - W:]]
    add x2 -> x0, other arithmetic: 1.5 us -> none  [the longest x1 0.86 us: per_device(): mine + lax.ppermute(piece(k), 'seq', [(s, (s + k) % count) for s in range...]
    dynamic_slice x1 -> x0, local copies, waits for them, and re-layouts: 0.93 us -> none  [per_device(): lax.dynamic_slice_in_dim(grad, (rank + k) % count * share, share, 0)]
  transfers between devices with their start and end apart: 8 -> 0, of which waited for: 4 -> 0; matrix products, arithmetic and copies ran while one was open for 3% -> 0% of each run, Pallas kernels for 0% -> 0%
where the time goes in v2:
time: 71.9 us; the launch traced here: 71.6 us
  Pallas kernels  69.4 us (97%)
  local copies, waits for them, and re-layouts  1.49 us (2%)
    pallas_call x1, Pallas kernels, per_device(): pl.pallas_call(functools.partial(main_kernel, tokens_here, heads, inner,...  42.4 us
    pallas_call x1, Pallas kernels, per_device(): pl.pallas_call(functools.partial(first_kernel, count, heads, inner, steps...  18 us
    pallas_call x1, Pallas kernels, per_device(): pl.pallas_call(functools.partial(last_kernel, count), in_specs=[vmem, vme...  8.98 us
    reshape x1, local copies, waits for them, and re-layouts, per_device(): mine.reshape(share, heads, hd)  1.49 us

profile of v2, /device:TPU:0, one launch (start us, length us, event | category | flops | bytes accessed | tf_op | source)
XLA Modules:
  0.0 71.6 jit_solution(16634365998076907248)
XLA Ops:
  0.6 18.0 %features.1 = (bf16[16384,128]{1,0:T(8,128)(2,1)}, bf16[4096,128]{1,0:T(8,128)(2,1)}, bf16[512,128]{1,0:T(8,128)(2,1)}, bf16[512,128]{1,0:T(8,128)(2,1)}, f32[128,128]{1,0:T(8,128)}) custom-call(bf16[16384,128]{1,0:T(8,128)(2,1)} %bitcast.5, bf16[512,128]{1,0:T(8,128)(2,1)} %bitcast.8, bf16[4096,128]{1,0:T(8,128)(2,1)} %k_ref.3, bf16[4096,128]{1,0:T(8,128)(2,1)} %v_ref.3, ...), custom_call_target="tpu_custom_call" | custom-call | tf_op jit(solution)/shard_map/features/pallas_call | solution.py:281
  18.7 42.4 %attention.1 = (bf16[16384,128]{1,0:T(8,128)(2,1)}, bf16[16384,128]{1,0:T(8,128)(2,1)}, f32[4,32,512]{2,1,0:T(8,128)}, bf16[4,32,512]{2,1,0:T(8,128)(2,1)}) custom-call(bf16[16384,128]{1,0:T(8,128)(2,1)} %bitcast.6, bf16[16384,128]{1,0:T(8,128)(2,1)} %get-tuple-element.12.qf_ref, bf16[16384,128]{1,0:T(8,128)(2,1)} %bitcast.7, bf16[4096,128]{1,0:T(8,128)(2,1)} %k_ref.3, ...), custom_call_target="tpu_custom_call" | custom-call | tf_op jit(solution)/shard_map/attention/pallas_call | solution.py:302
  61.1 9.0 %map_gradient.1 = f32[32,512]{1,0:T(8,128)} custom-call(f32[4,32,512]{2,1,0:T(8,128)} %get-tuple-element.19.g_ref, bf16[4,32,512]{2,1,0:T(8,128)(2,1)} %get-tuple-element.20.g16_ref), custom_call_target="tpu_custom_call" | custom-call | tf_op jit(solution)/shard_map/map_gradient/pallas_call | solution.py:325
  70.1 1.5 %reshape.29 = f32[32,4,128]{2,1,0:T(4,128)} reshape(f32[32,512]{1,0:T(8,128)} %map_gradient.1) | data formatting | bytes 131072 | tf_op jit(solution)/shard_map/reshape | solution.py:337

commit v3 on v2

--- a/solution.py
+++ b/solution.py
@@ -24,11 +24,6 @@
     return jnp.dot(a, b, preferred_element_type=jnp.float32)
 
 
-def split_two(x):
-    high = x.astype(jnp.bfloat16)
-    return high, (x - high.astype(jnp.float32)).astype(jnp.bfloat16)
-
-
 def head_masks(rows, heads, inner, hd):
     def mask(parts, of_head):
         shape = (rows, parts * hd)
@@ -37,6 +32,32 @@
         return jnp.where(of_head(head) == part, 1.0, 0.0).astype(jnp.bfloat16)
 
     return mask(heads // inner, lambda h: h // inner), mask(inner, lambda h: h % inner)
+
+
+def ahead_of(rows, start, heads):
+    shape = (rows, TILE)
+    local = (lax.broadcasted_iota(jnp.int32, shape, 0) + start) // heads
+    return local, lax.broadcasted_iota(jnp.int32, shape, 1) > local
+
+
+def window_softmax(q, k_win, v_win, ahead, invalid=None):
+    hd = q.shape[1]
+    mids = W // TILE
+    scale = hd ** (-0.5) * 1.4426950408889634
+    scores = nt(q, k_win)
+    parts = [scores[:, j * TILE : (j + 1) * TILE] for j in range(mids + 1)]
+    if invalid is not None:
+        parts = [p + invalid[j] if j < mids else p for j, p in enumerate(parts)]
+    kept = [jnp.where(ahead, parts[0], parts[mids])] + parts[1:mids]
+    highest = jnp.max(functools.reduce(jnp.maximum, kept), axis=1, keepdims=True)
+    kept = [jnp.exp2((p - highest) * scale) for p in kept]
+    weights = jnp.concatenate(
+        [jnp.where(ahead, kept[0], 0.0).astype(jnp.bfloat16)]
+        + [p.astype(jnp.bfloat16) for p in kept[1:]]
+        + [jnp.where(ahead, 0.0, kept[0]).astype(jnp.bfloat16)], 1
+    )
+    soft = nn(weights, v_win)
+    return (soft[:, :hd] / soft[:, hd:]).astype(jnp.bfloat16)
 
 
 def seq_barrier(rank, count):
@@ -49,10 +70,10 @@
 
 
 def first_kernel(
-    count, heads, inner, steps,
-    q_ref, maps_ref, k_ref, v_ref, key_map_ref,
-    qf_ref, kf_ref, rim_k_ref, rim_v_ref, prefix_ref,
-    outer_mask, local_sum, sums, halo, sum_send, sum_recv, halo_send, halo_recv,
+    count, heads, inner, steps, late_tile,
+    q_ref, late_q_ref, maps_ref, k_ref, v_ref, key_map_ref,
+    qf_ref, late_soft_ref, kf_ref, rim_k_ref, rim_v_ref, prefix_ref,
+    v_ones, outer_mask, local_sum, sums, halo, sum_send, sum_recv, halo_send, halo_recv,
 ):
     step = pl.program_id(0)
     rank = lax.axis_index("seq")
@@ -85,6 +106,8 @@
         kf_ref[...] = nn(k_ref[...], key_map_ref[...]).astype(jnp.bfloat16)
         local_sum[...] = tn(kf_ref[...], v_ref[...])
         outer_mask[...] = head_masks(rows, heads, inner, hd)[0]
+        v_ones[:, :hd] = v_ref[...]
+        v_ones[:, hd:] = jnp.ones((tokens, hd), jnp.bfloat16)
         pl.semaphore_wait(barrier, count - 1)
         for k in range(1, count):
             @pl.when(rank + k < count)
@@ -110,6 +133,18 @@
         for b in range(1, inner):
             qf = jnp.where(inner_head == b, spread[:, b * hd : (b + 1) * hd], qf)
         qf_ref[start : start + rows, :] = qf.astype(jnp.bfloat16)
+
+    tile_rows = TILE * heads
+    tiles = late_q_ref.shape[0] // tile_rows
+    for tile in range(tiles):
+        first = pl.multiple_of((late_tile + step * tiles + tile) * TILE - W, TILE)
+        k_win = k_ref[pl.ds(first, W + TILE), :]
+        v_win = v_ones[pl.ds(first, W + TILE), :]
+        for sub in range(0, tile_rows, rows):
+            start = tile * tile_rows + sub
+            late_soft_ref[start : start + rows, :] = window_softmax(
+                late_q_ref[start : start + rows, :], k_win, v_win, ahead_of(rows, sub, heads)[1]
+            )
 
     @pl.when(step == steps - 1)
     def _():
@@ -159,12 +194,14 @@
     for k, copy in enumerate(copies):
         copy.wait()
         total = total + slots[k].astype(jnp.float32)
-    out_ref[...] = total
+    hd = out_ref.shape[2]
+    for h in range(out_ref.shape[1]):
+        out_ref[:, h, :] = total[:, h * hd : (h + 1) * hd]
 
 
 def main_kernel(
-    tokens_here, heads, inner, tiles, rows_sub, steps,
-    q_ref, qf_ref, c_ref, k_ref, v_ref, kf_ref, rim_k_ref, rim_v_ref, prefix_ref,
+    tokens_here, heads, inner, tiles, rows_sub, steps, early,
+    q_ref, qf_ref, c_ref, late_soft_ref, k_ref, v_ref, kf_ref, rim_k_ref, rim_v_ref, prefix_ref,
     soft_ref, linear_ref, grad_ref, grad16_ref,
     k_ext, v_ext, outer_mask, inner_mask, state, grad,
 ):
@@ -185,66 +222,61 @@
         state[...] = prefix_ref[...]
         grad[...] = jnp.zeros_like(grad)
 
-    scale = hd ** (-0.5) * 1.4426950408889634
     zero = jnp.zeros((TILE, hd), jnp.bfloat16)
     mids = W // TILE
-    for tile in range(tiles):
-        index = step * tiles + tile
-        first = pl.multiple_of(index * TILE, TILE)
-        k_win = k_ext[pl.ds(first, W + TILE), :]
-        v_win = v_ext[pl.ds(first, W + TILE), :]
-        kf = kf_ref[pl.ds(first, TILE), :]
-        v = v_ref[pl.ds(first, TILE), :]
-        s_now = state[...]
-        s_hi, s_lo = split_two(s_now)
-        t_hi, t_lo = split_two(s_now.T)
-
-        def diagonal(a, b):
-            return jnp.concatenate(
-                [jnp.concatenate([a, zero], 1), jnp.concatenate([zero, b], 1)], 0
-            )
-
-        into_scores = diagonal(kf, v)
-        from_scores = jnp.concatenate([diagonal(v, kf), diagonal(s_hi, t_hi), diagonal(s_lo, t_lo)], 0)
-        invalid = [
-            jnp.where((rank == 0) & (index + j < mids), -1e30, 0.0).astype(jnp.float32)
-            for j in range(mids)
-        ]
-        queries, gradients = [], []
-        for sub in range(rows // rows_sub):
-            start = tile * rows + sub * rows_sub
-            q = q_ref[start : start + rows_sub, :]
-            c = c_ref[start : start + rows_sub, :]
-            shape = (rows_sub, TILE)
-            local = (lax.broadcasted_iota(jnp.int32, shape, 0) + sub * rows_sub) // heads
-            ahead = lax.broadcasted_iota(jnp.int32, shape, 1) > local
-            scores = nt(q, k_win)
-            parts = [scores[:, j * TILE : (j + 1) * TILE] for j in range(mids + 1)]
-            parts = [p + invalid[j] if j < mids else p for j, p in enumerate(parts)]
-            both = jnp.where(ahead, parts[0], parts[mids])
-            kept = [both] + parts[1:mids]
-            highest = jnp.max(functools.reduce(jnp.maximum, kept), axis=1, keepdims=True)
-            kept = [jnp.exp2((p - highest) * scale) for p in kept]
-            weights = jnp.concatenate(
-                [jnp.where(ahead, kept[0], 0.0).astype(jnp.bfloat16)]
-                + [p.astype(jnp.bfloat16) for p in kept[1:]]
-                + [jnp.where(ahead, 0.0, kept[0]).astype(jnp.bfloat16)], 1
-            )
-            soft = nn(weights, v_win)
-            soft_ref[start : start + rows_sub, :] = (soft[:, :hd] / soft[:, hd:]).astype(jnp.bfloat16)
-            pair = jnp.concatenate([qf_ref[start : start + rows_sub, :], c], 1)
-            pair_scores = nt(pair, into_scores)
-            ahead_two = jnp.concatenate([ahead, ahead], 1)
-            pair_scores = jnp.where(ahead_two, 0.0, pair_scores).astype(jnp.bfloat16)
-            pair_out = nn(jnp.concatenate([pair_scores, pair, pair], 1), from_scores)
-            position = rank * tokens_here + index * TILE + local + 1
-            factor = lax.rsqrt(position.astype(jnp.float32))
-            linear_ref[start : start + rows_sub, :] = (factor * pair_out[:, :hd]).astype(jnp.bfloat16)
-            fg = (factor * pair_out[:, hd:]).astype(jnp.bfloat16)
-            queries.append(jnp.concatenate([q] * outer, 1) * outer_mask[...])
-            gradients.append(jnp.concatenate([fg] * inner, 1) * inner_mask[...])
-        grad[...] += tn(jnp.concatenate(queries, 0), jnp.concatenate(gradients, 0))
-        state[...] = s_now + tn(kf, v)
+
+    def block(with_softmax):
+        for tile in range(tiles):
+            index = step * tiles + tile
+            first = pl.multiple_of(index * TILE, TILE)
+            k_win = k_ext[pl.ds(first, W + TILE), :]
+            v_win = v_ext[pl.ds(first, W + TILE), :]
+            kf = kf_ref[pl.ds(first, TILE), :]
+            v = v_ref[pl.ds(first, TILE), :]
+            s_now = state[...]
+
+            def diagonal(a, b):
+                return jnp.concatenate(
+                    [jnp.concatenate([a, zero], 1), jnp.concatenate([zero, b], 1)], 0
+                )
+
+            into_scores = diagonal(kf, v)
+            carried = diagonal(s_now.astype(jnp.bfloat16), s_now.T.astype(jnp.bfloat16))
+            from_scores = jnp.concatenate([diagonal(v, kf), carried], 0)
+            invalid = [
+                jnp.where((rank == 0) & (index + j < mids), -1e30, 0.0).astype(jnp.float32)
+                for j in range(mids)
+            ]
+            queries, gradients = [], []
+            for sub in range(rows // rows_sub):
+                start = tile * rows + sub * rows_sub
+                q = q_ref[start : start + rows_sub, :]
+                c = c_ref[start : start + rows_sub, :]
+                local, ahead = ahead_of(rows_sub, sub * rows_sub, heads)
+                if with_softmax:
+                    soft_ref[start : start + rows_sub, :] = window_softmax(q, k_win, v_win, ahead, invalid)
+                pair = jnp.concatenate([qf_ref[start : start + rows_sub, :], c], 1)
+                pair_scores = nt(pair, into_scores)
+                ahead_two = jnp.concatenate([ahead, ahead], 1)
+                pair_scores = jnp.where(ahead_two, 0.0, pair_scores).astype(jnp.bfloat16)
+                pair_out = nn(jnp.concatenate([pair_scores, pair], 1), from_scores)
+                position = rank * tokens_here + index * TILE + local + 1
+                factor = lax.rsqrt(position.astype(jnp.float32))
+                linear_ref[start : start + rows_sub, :] = (factor * pair_out[:, :hd]).astype(jnp.bfloat16)
+                fg = (factor * pair_out[:, hd:]).astype(jnp.bfloat16)
+                queries.append(jnp.concatenate([q] * outer, 1) * outer_mask[...])
+                gradients.append(jnp.concatenate([fg] * inner, 1) * inner_mask[...])
+            grad[...] += tn(jnp.concatenate(queries, 0), jnp.concatenate(gradients, 0))
+            state[...] = s_now + tn(kf, v)
+
+    @pl.when(step < early)
+    def _():
+        block(True)
+
+    @pl.when(step >= early)
+    def _():
+        soft_ref[...] = late_soft_ref[...]
+        block(False)
 
     @pl.when(step == steps - 1)
     def _():
@@ -267,6 +299,8 @@
     step_rows = TILE * tiles * heads
     total = tokens_here * heads
     steps = total // step_rows
+    early = steps // 2
+    late_rows = (steps - early) * step_rows // steps
     whole = lambda a: pl.BlockSpec(a.shape, lambda i: (0,) * len(a.shape))
     rows_spec = pl.BlockSpec((step_rows, hd), lambda i: (i, 0))
     maps = query_maps.reshape(heads * hd, hd)
@@ -274,17 +308,21 @@
     cotangent = linear_cotangent.reshape(total, hd)
 
     rows16 = jax.ShapeDtypeStruct((total, hd), jnp.bfloat16)
+    late16 = jax.ShapeDtypeStruct((steps * late_rows, hd), jnp.bfloat16)
     kf16 = jax.ShapeDtypeStruct((tokens_here, hd), jnp.bfloat16)
     rim = jax.ShapeDtypeStruct((W, hd), jnp.bfloat16)
     square = jax.ShapeDtypeStruct((hd, hd), jnp.float32)
     dma = pltpu.SemaphoreType.DMA
-    query_features, key_features, rim_keys, rim_values, prefix = pl.pallas_call(
-        functools.partial(first_kernel, count, heads, inner, steps),
+    query_features, late_soft, key_features, rim_keys, rim_values, prefix = pl.pallas_call(
+        functools.partial(first_kernel, count, heads, inner, steps, early * tiles),
         grid=(steps,),
-        in_specs=[rows_spec] + [whole(a) for a in (maps, keys, values, key_map)],
-        out_specs=[rows_spec] + [whole(a) for a in (kf16, rim, rim, square)],
-        out_shape=[rows16, kf16, rim, rim, square],
+        in_specs=[rows_spec, pl.BlockSpec((late_rows, hd), lambda i: (i + early * step_rows // late_rows, 0))]
+        + [whole(a) for a in (maps, keys, values, key_map)],
+        out_specs=[rows_spec, pl.BlockSpec((late_rows, hd), lambda i: (i, 0))]
+        + [whole(a) for a in (kf16, rim, rim, square)],
+        out_shape=[rows16, late16, kf16, rim, rim, square],
         scratch_shapes=[
+            pltpu.VMEM((tokens_here, 2 * hd), jnp.bfloat16),
             pltpu.VMEM((rows_sub, outer * hd), jnp.bfloat16),
             pltpu.VMEM((hd, hd), jnp.float32),
             pltpu.VMEM((count - 1, hd, hd), jnp.float32),
@@ -295,14 +333,16 @@
             dimension_semantics=("arbitrary",), collective_id=0, has_side_effects=True
         ),
         name="features",
-    )(queries, maps, keys, values, key_map)
+    )(queries, queries, maps, keys, values, key_map)
 
     pieces = (count, share, heads * hd)
     small = (keys, values, key_features, rim_keys, rim_values, prefix)
     soft, linear, grad, grad16 = pl.pallas_call(
-        functools.partial(main_kernel, tokens_here, heads, inner, tiles, rows_sub, steps),
+        functools.partial(main_kernel, tokens_here, heads, inner, tiles, rows_sub, steps, early),
         grid=(steps,),
-        in_specs=[rows_spec] * 3 + [whole(a) for a in small],
+        in_specs=[rows_spec] * 3
+        + [pl.BlockSpec((step_rows, hd), lambda i: (jnp.maximum(i - early, 0), 0))]
+        + [whole(a) for a in small],
         out_specs=[rows_spec] * 2 + [pl.BlockSpec(pieces, lambda i: (0, 0, 0))] * 2,
         out_shape=[
             rows16, rows16,
@@ -319,14 +359,14 @@
         ],
         compiler_params=pltpu.CompilerParams(dimension_semantics=("arbitrary",)),
         name="attention",
-    )(queries, query_features, cotangent, *small)
+    )(queries, query_features, cotangent, late_soft, *small)
 
     vmem = pl.BlockSpec(memory_space=pltpu.VMEM)
     mine = pl.pallas_call(
         functools.partial(last_kernel, count),
         in_specs=[vmem, vmem],
         out_specs=vmem,
-        out_shape=jax.ShapeDtypeStruct(pieces[1:], jnp.float32),
+        out_shape=jax.ShapeDtypeStruct((share, heads, hd), jnp.float32),
         scratch_shapes=[
             pltpu.VMEM((count - 1,) + pieces[1:], jnp.bfloat16), dma((count - 1,)), dma((count - 1,)),
         ],
@@ -334,7 +374,7 @@
         name="map_gradient",
     )(grad, grad16)
     shape = (tokens_here, heads, hd)
-    return soft.reshape(shape), linear.reshape(shape), mine.reshape(share, heads, hd)
+    return soft.reshape(shape), linear.reshape(shape), mine
 
 
 def solution(mesh):

time: 71.9 us -> 65 us (0.904)
  Pallas kernels: 69.4 us -> 62.7 us
    pallas_call x1, Pallas kernels: 42.4 us -> 32.6 us  [per_device(): pl.pallas_call(functools.partial(main_kernel, tokens_here, heads, inner,...]
    pallas_call x1, Pallas kernels: 18 us -> 22.6 us  [per_device(): pl.pallas_call(functools.partial(first_kernel, count, heads, inner, steps...]
    pallas_call x1, Pallas kernels: 8.98 us -> 7.43 us  [per_device(): pl.pallas_call(functools.partial(last_kernel, count), in_specs=[vmem, vme...]
    reshape x1 -> x0, local copies, waits for them, and re-layouts: 1.49 us -> none  [per_device(): mine.reshape(share, heads, hd)]
    unnamed x0 -> x1, local copies, waits for them, and re-layouts: none -> 1.47 us
where the time goes in v3:
time: 65 us; the launch traced here: 64.8 us
  Pallas kernels  62.7 us (96%)
  local copies, waits for them, and re-layouts  1.47 us (2%)
  between operations  0.65 us (1%)
    pallas_call x1, Pallas kernels, per_device(): pl.pallas_call(functools.partial(main_kernel, tokens_here, heads, inner,...  32.6 us
    pallas_call x1, Pallas kernels, per_device(): pl.pallas_call(functools.partial(first_kernel, count, heads, inner, steps...  22.6 us
    pallas_call x1, Pallas kernels, per_device(): pl.pallas_call(functools.partial(last_kernel, count), in_specs=[vmem, vme...  7.43 us
    unnamed x1, local copies, waits for them, and re-layouts  1.47 us

profile of v3, /device:TPU:0, one launch (start us, length us, event | category | flops | bytes accessed | tf_op | source)
XLA Modules:
  0.0 64.8 jit_solution(10333566101096800672)
XLA Ops:
  0.6 22.6 %features.1 = (bf16[16384,128]{1,0:T(8,128)(2,1)}, bf16[8192,128]{1,0:T(8,128)(2,1)}, bf16[4096,128]{1,0:T(8,128)(2,1)}, bf16[512,128]{1,0:T(8,128)(2,1)}, bf16[512,128]{1,0:T(8,128)(2,1)}, /*index=5*/f32[128,128]{1,0:T(8,128)}) custom-call(bf16[16384,128]{1,0:T(8,128)(2,1)} %bitcast.5, bf16[16384,128]{1,0:T(8,128)(2,1)} %bitcast.6, ...), custom_call_target="tpu_custom_call" | custom-call | tf_op jit(solution)/shard_map/features/pallas_call | solution.py:316
  23.3 32.6 %attention.1 = (bf16[16384,128]{1,0:T(8,128)(2,1)}, bf16[16384,128]{1,0:T(8,128)(2,1)}, f32[4,32,512]{2,1,0:T(8,128)}, bf16[4,32,512]{2,1,0:T(8,128)(2,1)}) custom-call(bf16[16384,128]{1,0:T(8,128)(2,1)} %bitcast.7, bf16[16384,128]{1,0:T(8,128)(2,1)} %get-tuple-element.13.qf_ref, bf16[16384,128]{1,0:T(8,128)(2,1)} %bitcast.8, ...), custom_call_target="tpu_custom_call" | custom-call | tf_op jit(solution)/shard_map/attention/pallas_call | solution.py:340
  55.9 7.4 %map_gradient.1 = f32[32,4,128]{2,1,0:T(4,128)} custom-call(f32[4,32,512]{2,1,0:T(8,128)} %get-tuple-element.21.g_ref, bf16[4,32,512]{2,1,0:T(8,128)(2,1)} %get-tuple-element.22.g16_ref), custom_call_target="tpu_custom_call" | custom-call | tf_op jit(solution)/shard_map/map_gradient/pallas_call | solution.py:365
  63.4 1.5 %copy.10 = f32[32,4,128]{2,1,0:T(4,128)} copy(f32[32,4,128]{2,1,0:T(4,128)} %map_gradient.1) | data formatting | bytes 131072

commit v4 on v3

--- a/solution.py
+++ b/solution.py
@@ -295,7 +295,7 @@
     outer = heads // inner
     share = hd // count
     tiles = 4
-    rows_sub = min(256, TILE * heads)
+    rows_sub = min(512, TILE * heads)
     step_rows = TILE * tiles * heads
     total = tokens_here * heads
     steps = total // step_rows

time: 65 us -> 57.9 us (0.89)
  Pallas kernels: 62.7 us -> 55.6 us
    pallas_call x1, Pallas kernels: 32.6 us -> 27.3 us  [per_device(): pl.pallas_call(functools.partial(main_kernel, tokens_here, heads, inner,...]
    pallas_call x1, Pallas kernels: 22.6 us -> 20.9 us  [per_device(): pl.pallas_call(functools.partial(first_kernel, count, heads, inner, steps...]
where the time goes in v4:
time: 57.9 us; the launch traced here: 57.7 us
  Pallas kernels  55.6 us (96%)
  local copies, waits for them, and re-layouts  1.47 us (3%)
  between operations  0.65 us (1%)
    pallas_call x1, Pallas kernels, per_device(): pl.pallas_call(functools.partial(main_kernel, tokens_here, heads, inner,...  27.3 us
    pallas_call x1, Pallas kernels, per_device(): pl.pallas_call(functools.partial(first_kernel, count, heads, inner, steps...  20.9 us
    pallas_call x1, Pallas kernels, per_device(): pl.pallas_call(functools.partial(last_kernel, count), in_specs=[vmem, vme...  7.43 us
    unnamed x1, local copies, waits for them, and re-layouts  1.47 us

profile of v4, /device:TPU:0, one launch (start us, length us, event | category | flops | bytes accessed | tf_op | source)
XLA Modules:
  0.0 57.7 jit_solution(3533731852223571415)
XLA Ops:
  0.6 20.9 %features.1 = (bf16[16384,128]{1,0:T(8,128)(2,1)}, bf16[8192,128]{1,0:T(8,128)(2,1)}, bf16[4096,128]{1,0:T(8,128)(2,1)}, bf16[512,128]{1,0:T(8,128)(2,1)}, bf16[512,128]{1,0:T(8,128)(2,1)}, /*index=5*/f32[128,128]{1,0:T(8,128)}) custom-call(bf16[16384,128]{1,0:T(8,128)(2,1)} %bitcast.5, bf16[16384,128]{1,0:T(8,128)(2,1)} %bitcast.6, ...), custom_call_target="tpu_custom_call" | custom-call | tf_op jit(solution)/shard_map/features/pallas_call | solution.py:316
  21.5 27.3 %attention.1 = (bf16[16384,128]{1,0:T(8,128)(2,1)}, bf16[16384,128]{1,0:T(8,128)(2,1)}, f32[4,32,512]{2,1,0:T(8,128)}, bf16[4,32,512]{2,1,0:T(8,128)(2,1)}) custom-call(bf16[16384,128]{1,0:T(8,128)(2,1)} %bitcast.7, bf16[16384,128]{1,0:T(8,128)(2,1)} %get-tuple-element.13.qf_ref, bf16[16384,128]{1,0:T(8,128)(2,1)} %bitcast.8, ...), custom_call_target="tpu_custom_call" | custom-call | tf_op jit(solution)/shard_map/attention/pallas_call | solution.py:340
  48.8 7.4 %map_gradient.1 = f32[32,4,128]{2,1,0:T(4,128)} custom-call(f32[4,32,512]{2,1,0:T(8,128)} %get-tuple-element.21.g_ref, bf16[4,32,512]{2,1,0:T(8,128)(2,1)} %get-tuple-element.22.g16_ref), custom_call_target="tpu_custom_call" | custom-call | tf_op jit(solution)/shard_map/map_gradient/pallas_call | solution.py:365
  56.2 1.5 %copy.10 = f32[32,4,128]{2,1,0:T(4,128)} copy(f32[32,4,128]{2,1,0:T(4,128)} %map_gradient.1) | data formatting | bytes 131072

commit v5 on v4

--- a/solution.py
+++ b/solution.py
@@ -70,11 +70,14 @@
 
 
 def first_kernel(
-    count, heads, inner, steps, late_tile,
-    q_ref, late_q_ref, maps_ref, k_ref, v_ref, key_map_ref,
+    count, heads, inner, steps, late_tile, tiles, q_ref, *refs,
+):
+    late_q_refs, refs = refs[:tiles], refs[tiles:]
+    (
+    maps_ref, k_ref, v_ref, key_map_ref,
     qf_ref, late_soft_ref, kf_ref, rim_k_ref, rim_v_ref, prefix_ref,
     v_ones, outer_mask, local_sum, sums, halo, sum_send, sum_recv, halo_send, halo_recv,
-):
+    ) = refs
     step = pl.program_id(0)
     rank = lax.axis_index("seq")
     tokens, hd = k_ref.shape
@@ -135,7 +138,6 @@
         qf_ref[start : start + rows, :] = qf.astype(jnp.bfloat16)
 
     tile_rows = TILE * heads
-    tiles = late_q_ref.shape[0] // tile_rows
     for tile in range(tiles):
         first = pl.multiple_of((late_tile + step * tiles + tile) * TILE - W, TILE)
         k_win = k_ref[pl.ds(first, W + TILE), :]
@@ -143,7 +145,7 @@
         for sub in range(0, tile_rows, rows):
             start = tile * tile_rows + sub
             late_soft_ref[start : start + rows, :] = window_softmax(
-                late_q_ref[start : start + rows, :], k_win, v_win, ahead_of(rows, sub, heads)[1]
+                late_q_refs[tile][sub : sub + rows, :], k_win, v_win, ahead_of(rows, sub, heads)[1]
             )
 
     @pl.when(step == steps - 1)
@@ -299,8 +301,9 @@
     step_rows = TILE * tiles * heads
     total = tokens_here * heads
     steps = total // step_rows
-    early = steps // 2
-    late_rows = (steps - early) * step_rows // steps
+    early = steps // 4
+    late_tiles = (steps - early) * tiles // steps
+    late_rows = late_tiles * TILE * heads
     whole = lambda a: pl.BlockSpec(a.shape, lambda i: (0,) * len(a.shape))
     rows_spec = pl.BlockSpec((step_rows, hd), lambda i: (i, 0))
     maps = query_maps.reshape(heads * hd, hd)
@@ -314,9 +317,13 @@
     square = jax.ShapeDtypeStruct((hd, hd), jnp.float32)
     dma = pltpu.SemaphoreType.DMA
     query_features, late_soft, key_features, rim_keys, rim_values, prefix = pl.pallas_call(
-        functools.partial(first_kernel, count, heads, inner, steps, early * tiles),
+        functools.partial(first_kernel, count, heads, inner, steps, early * tiles, late_tiles),
         grid=(steps,),
-        in_specs=[rows_spec, pl.BlockSpec((late_rows, hd), lambda i: (i + early * step_rows // late_rows, 0))]
+        in_specs=[rows_spec]
+        + [
+            pl.BlockSpec((TILE * heads, hd), lambda i, j=j: (early * tiles + i * late_tiles + j, 0))
+            for j in range(late_tiles)
+        ]
         + [whole(a) for a in (maps, keys, values, key_map)],
         out_specs=[rows_spec, pl.BlockSpec((late_rows, hd), lambda i: (i, 0))]
         + [whole(a) for a in (kf16, rim, rim, square)],
@@ -333,7 +340,7 @@
             dimension_semantics=("arbitrary",), collective_id=0, has_side_effects=True
         ),
         name="features",
-    )(queries, queries, maps, keys, values, key_map)
+    )(queries, *[queries] * late_tiles, maps, keys, values, key_map)
 
     pieces = (count, share, heads * hd)
     small = (keys, values, key_features, rim_keys, rim_values, prefix)

time: 57.9 us -> 62.8 us (1.085)
  Pallas kernels: 55.6 us -> 60.5 us
    pallas_call x1, Pallas kernels: 20.9 us -> 28.6 us  [per_device(): pl.pallas_call(functools.partial(first_kernel, count, heads, inner, steps...]
    pallas_call x1, Pallas kernels: 27.3 us -> 24.5 us  [per_device(): pl.pallas_call(functools.partial(main_kernel, tokens_here, heads, inner,...]
where the time goes in v5:
time: 62.8 us; the launch traced here: 62.6 us
  Pallas kernels  60.5 us (96%)
  local copies, waits for them, and re-layouts  1.47 us (2%)
  between operations  0.65 us (1%)
    pallas_call x1, Pallas kernels, per_device(): pl.pallas_call(functools.partial(first_kernel, count, heads, inner, steps...  28.6 us
    pallas_call x1, Pallas kernels, per_device(): pl.pallas_call(functools.partial(main_kernel, tokens_here, heads, inner,...  24.5 us
    pallas_call x1, Pallas kernels, per_device(): pl.pallas_call(functools.partial(last_kernel, count), in_specs=[vmem, vme...  7.43 us
    unnamed x1, local copies, waits for them, and re-layouts  1.47 us

profile of v5, /device:TPU:0, one launch (start us, length us, event | category | flops | bytes accessed | tf_op | source)
XLA Modules:
  0.0 62.6 jit_solution(2703030873028264099)
XLA Ops:
  0.6 28.6 %features.1 = (bf16[16384,128]{1,0:T(8,128)(2,1)}, bf16[12288,128]{1,0:T(8,128)(2,1)}, bf16[4096,128]{1,0:T(8,128)(2,1)}, bf16[512,128]{1,0:T(8,128)(2,1)}, bf16...) custom-call(bf16[16384,128]{1,0:T(8,128)(2,1)} %bitcast.5, bf16[16384,128]{1,0:T(8,128)(2,1)} %bitcast.6, ...), custom_call_target="tpu_custom_call" | custom-call | tf_op jit(solution)/shard_map/features/pallas_call | solution.py:319
  29.2 24.5 %attention.1 = (bf16[16384,128]{1,0:T(8,128)(2,1)}, bf16[16384,128]{1,0:T(8,128)(2,1)}, f32[4,32,512]{2,1,0:T(8,128)}, bf16[4,32,512]{2,1,0:T(8,128)(2,1)}) custom-call(bf16[16384,128]{1,0:T(8,128)(2,1)} %bitcast.9, bf16[16384,128]{1,0:T(8,128)(2,1)} %get-tuple-element.13.qf_ref, bf16[16384,128]{1,0:T(8,128)(2,1)} %bitcast.10, ...), custom_call_target="tpu_custom_call" | custom-call | tf_op jit(solution)/shard_map/attention/pallas_call | solution.py:347
  53.7 7.4 %map_gradient.1 = f32[32,4,128]{2,1,0:T(4,128)} custom-call(f32[4,32,512]{2,1,0:T(8,128)} %get-tuple-element.21.g_ref, bf16[4,32,512]{2,1,0:T(8,128)(2,1)} %get-tuple-element.22.g16_ref), custom_call_target="tpu_custom_call" | custom-call | tf_op jit(solution)/shard_map/map_gradient/pallas_call | solution.py:372
  61.1 1.5 %copy.10 = f32[32,4,128]{2,1,0:T(4,128)} copy(f32[32,4,128]{2,1,0:T(4,128)} %map_gradient.1) | data formatting | bytes 131072
